TPU v7x, 128 devices: a whole 4x4x4 slice. The times are simulated.
128 devices in a mesh: fsdp: 32 (over y, x_hi, z), red: 4 (over x_lo, core).
Axes of the slice: x: 4 (x_hi: 2, x_lo: 2; x = x_hi * 2 + x_lo), y: 4, z: 4, core: 2. Of those that a mesh axis runs over, the one named last changes fastest.
Arguments:
- layer_input: bfloat16 [2, 8192, 16384], P(None, 'fsdp', 'red'), may hold values from -6 to 6
- kv_cotangent: bfloat16 [2, 8192, 1024], P(None, 'fsdp'), may hold values from -16 to 16
- failed_member: int32 [32], P('fsdp'), may hold values from 0 to 4
- master: float32 [2, 1024, 16384], P(None, 'fsdp', 'red'), may hold values from -0.046875 to 0.046875
- first_moment: float32 [2, 1024, 16384], P(None, 'fsdp', 'red'), may hold values from -4 to 4
- second_moment: float32 [2, 1024, 16384], P(None, 'fsdp', 'red'), may hold values from 0.05 to 2
- loss_scale: float32 [32, 4], P('fsdp', 'red'), may hold values from 2 to 8
- spare_master: float32 [2, 1024, 16384], P(None, 'fsdp', 'red'), may hold values from -0.046875 to 0.046875
- spare_first: float32 [2, 1024, 16384], P(None, 'fsdp', 'red'), may hold values from -4 to 4
- spare_second: float32 [2, 1024, 16384], P(None, 'fsdp', 'red'), may hold values from 0.05 to 2
- spare_scale: float32 [32, 4], P('fsdp', 'red'), may hold values from 2 to 8
Outputs:
- kv_out: bfloat16 [2, 8192, 1024], P(None, 'fsdp', 'red')
- input_grad: bfloat16 [2, 8192, 16384], P(None, 'fsdp', 'red')
- new_master: float32 [2, 1024, 16384], P(None, 'fsdp', 'red')
- new_first: float32 [2, 1024, 16384], P(None, 'fsdp', 'red')
- new_second: float32 [2, 1024, 16384], P(None, 'fsdp', 'red')
Inputs may be any that keep to these rules, and one draw needn't show every extreme that they name: failed_member[f] is the member of redundancy group f (index along red) whose state was lost; the value 4 means that group lost nothing.
All inputs are finite; a program needn't handle non-finite values.
Results may differ from a plain program's by a relative error of at most 0.017.
Values may be sent and summed in bfloat16 or wider, within the bound.
A program may use at most 128 MiB of HBM per device.

v0:
```python
import functools

import jax
import jax.numpy as jnp
from jax import lax
from jax.sharding import Mesh
from jax.sharding import PartitionSpec as P

RED = ("red_0", "red_1")
FSDP = ("fsdp_0", "fsdp_1", "fsdp_2")
FSDP_RED = ("fsdp_0", "fsdp_1", "fsdp_2", "red_0", "red_1")


BETA_FIRST = 0.9
BETA_SECOND = 0.95
LEARN_RATE = 0.01
DECAY_RATE = 0.1
ADAM_EPS = 1e-08
MEAN_EPS = 1e-06


def shifted(shard, axis, by):
    length = lax.axis_size(axis)
    return lax.ppermute(shard, axis, [(i, (i + by) % length) for i in range(length)])


def cut_along(shard, dim, length):
    before, after = (shard.shape[:dim], shard.shape[dim + 1 :])
    return jnp.moveaxis(shard.reshape(*before, length, -1, *after), dim, 0)


def sent_and_summed(shard, axis, dim):
    length = lax.axis_size(axis)
    parts = lax.all_to_all(cut_along(shard, dim, length), axis, 0, 0, tiled=True)
    return jnp.sum(parts.astype(jnp.float32), axis=0)


def reduced_to_own(parts, axes, order):
    inside = parts.shape[1:]
    parts = parts.reshape(*(lax.axis_size(a) for a in axes), *inside)
    parts = jnp.moveaxis(parts, order, range(len(axes))).reshape(-1, *inside)
    for k in order:
        parts = lax.psum_scatter(parts, axes[k], scatter_dimension=0, tiled=True)
    return parts[0]


def summed_rows(shard, axes, order, dim):
    length = lax.axis_size(axes)
    return reduced_to_own(cut_along(shard, dim, length), axes, order)


def by_axis(shard, axes):
    return functools.reduce(lax.psum, axes, shard)


def local(
    layer_input,
    kv_cotangent,
    failed_member,
    master,
    first_moment,
    second_moment,
    loss_scale,
    spare_master,
    spare_first,
    spare_second,
    spare_scale,
):
    layers = master.shape[0]
    local_rows = master.shape[1]
    replaced = lax.axis_index(RED) == failed_member[0]
    copy_master, copy_first, copy_second, copy_scale = (
        shifted(spare_master.astype(jnp.bfloat16), RED, 1).astype(spare_master.dtype),
        shifted(spare_first.astype(jnp.bfloat16), RED, 1).astype(spare_first.dtype),
        shifted(spare_second.astype(jnp.bfloat16), RED, 1).astype(spare_second.dtype),
        shifted(spare_scale.astype(jnp.bfloat16), RED, 1).astype(spare_scale.dtype),
    )
    master_now = jnp.where(replaced, copy_master, master)
    first_now = jnp.where(replaced, copy_first, first_moment)
    second_now = jnp.where(replaced, copy_second, second_moment)
    scale_now = jnp.where(replaced, copy_scale, loss_scale)
    weights = master_now.astype(jnp.bfloat16)
    gathered = lax.all_gather(weights, FSDP, axis=1, tiled=True)
    kv_list = []
    input_list = []
    for layer_index in range(layers):
        inputs = layer_input[layer_index]
        upstream = kv_cotangent[layer_index]
        full_weight = gathered[layer_index]
        partial_kv = lax.dot_general(
            inputs, full_weight, (((1,), (1,)), ((), ())), preferred_element_type=jnp.float32
        )
        kv_list.append(
            sent_and_summed(partial_kv.astype(jnp.bfloat16), RED, 1).astype(jnp.bfloat16)
        )
        input_list.append(
            jnp.dot(upstream, full_weight, preferred_element_type=jnp.float32).astype(jnp.bfloat16)
        )
    grad_terms = jnp.einsum(
        "ltc,ltd->lcd", kv_cotangent, layer_input, preferred_element_type=jnp.float32
    )
    grad_sum = summed_rows(grad_terms.astype(jnp.bfloat16), FSDP, (0, 2, 1), 1).astype(jnp.float32)
    gradient = grad_sum / scale_now[0, 0]
    total_squares = by_axis(jnp.sum(gradient * gradient), FSDP_RED)
    entries = layers * local_rows * lax.axis_size(FSDP) * master.shape[2] * lax.axis_size(RED)
    factor = jnp.minimum(1.0, lax.rsqrt(total_squares / entries + MEAN_EPS))
    clipped = gradient * factor
    new_first = BETA_FIRST * first_now + (1.0 - BETA_FIRST) * clipped
    new_second = BETA_SECOND * second_now + (1.0 - BETA_SECOND) * clipped * clipped
    new_master = master_now - LEARN_RATE * (
        new_first / (jnp.sqrt(new_second) + ADAM_EPS) + DECAY_RATE * master_now
    )
    return (jnp.stack(kv_list), jnp.stack(input_list), new_master, new_first, new_second)


def solution(mesh):
    split = Mesh(
        mesh.devices.reshape(4, 2, 4, 2, 2), ("fsdp_0", "fsdp_1", "fsdp_2", "red_0", "red_1")
    )
    placed = (
        P(None, FSDP, RED),
        P(None, FSDP, None),
        P(FSDP),
        P(None, FSDP, RED),
        P(None, FSDP, RED),
        P(None, FSDP, RED),
        P(FSDP, RED),
        P(None, FSDP, RED),
        P(None, FSDP, RED),
        P(None, FSDP, RED),
        P(FSDP, RED),
    )
    return jax.shard_map(
        local,
        mesh=split,
        in_specs=placed,
        out_specs=(
            P(None, FSDP, RED),
            P(None, FSDP, RED),
            P(None, FSDP, RED),
            P(None, FSDP, RED),
            P(None, FSDP, RED),
        ),
        check_vma=False,
    )
```

profile of v0, /device:TPU:1, one launch (start us, length us, event | category | flops | bytes accessed | tf_op | source)
XLA Modules:
  0.0 370.0 jit_solution(7072015989123471790)
XLA Ops:
  8.0 0.0 reduce-scatter.4.cloned.1.call-start
  8.0 12.8 %convolution_convert_fusion = bf16[2,1024,4096]{2,1,0:T(8,128)(2,1)} fusion(bf16[2,256,1024]{2,1,0:T(8,128)(2,1)} %param.12, bf16[2,256,4096]{2,1,0:T(8,128)(2,1)} %param.11), kind=kOutput, calls=%fused_computation | convolution fusion | flops 4303355904 | bytes 22020096 | tf_op jit(solution)/shard_map/ltc,ltd->lcd/dot_general | solution.py:99
  20.8 14.0 %copy.20 = bf16[4,2,4,2,32,4096]{5,4,3,1,2,0:T(8,128)(2,1)} copy(bf16[4,2,4,2,32,4096]{5,4,2,1,0,3:T(8,128)(2,1)} %bitcast.78) | data formatting | bytes 33554432 | tf_op jit(solution)/shard_map/reshape | solution.py:40
  34.8 0.0 copy-start.2
  34.8 0.0 copy-start
  34.8 0.0 reduce-scatter.4.cloned.1.call-update
  34.9 0.0 all-gather.2.cloned.1.call-start
  34.9 1.1 copy-done.2
  36.1 0.1 convert_element_type.62
  36.1 2.7 collective-permute-start
  39.4 0.0 copy-start.3
  39.4 5.5 %collective-permute-done = bf16[2,32,4096]{2,1,0:T(8,128)(2,1)S(1)} collective-permute-done((bf16[2,32,4096]{2,1,0:T(8,128)(2,1)S(1)}, bf16[2,32,4096]{2,1,0:T(8,128)(2,1)S(1)}, u32[]{:S(2)}, u32[]{:S(2)}) %collective-permute-start) | collective-permute-done | bytes 524320 | tf_op jit(solution)/shard_map/ppermute | solution.py:24
  44.9 0.0 copy-done
  44.9 0.9 fusion.20
  45.8 0.0 all-gather.2.cloned.1.call-update
  45.8 0.0 reduce-scatter.6.cloned.1.call-start
  45.9 179.6 %reduce-scatter.4.cloned.1.call-done = bf16[8,2,32,4096]{3,2,1,0:T(8,128)(2,1)} async-done(((bf16[32,2,32,4096]{3,2,1,0:T(8,128)(2,1)}), bf16[8,2,32,4096]{3,2,1,0:T(8,128)(2,1)}) %reduce-scatter.4.cloned.1.call-update) | async-done | bytes 4194320 | tf_op jit(solution)/shard_map/reduce_scatter | solution.py:43
  225.5 0.0 reduce-scatter.6.cloned.1.call-update
  226.2 2.9 collective-permute-start.2
  229.1 2.1 convert_element_type.73
  231.2 0.1 collective-permute-start.1
  231.3 0.0 copy-done.3
  231.3 0.8 convert_element_type.79
  232.1 0.6 collective-permute-start.3
  233.4 0.0 collective-permute-done.2
  234.0 13.6 %all-gather.2.cloned.1.call-done = bf16[2,1024,4096]{2,1,0:T(8,128)(2,1)} async-done(((bf16[2,32,4096]{2,1,0:T(8,128)(2,1)}), bf16[2,1024,4096]{2,1,0:T(8,128)(2,1)}) %all-gather.2.cloned.1.call-update) | async-done | bytes 16777232 | tf_op jit(solution)/shard_map/all_gather | solution.py:83
  247.6 7.3 %fusion.12 = bf16[1024,256]{1,0:T(8,128)(2,1)} fusion(bf16[2,256,4096]{2,1,0:T(8,128)(2,1)} %param.11, bf16[2,1024,4096]{2,1,0:T(8,128)(2,1)} %all-gather.2.cloned.1.call-done), kind=kOutput, calls=%fused_computation.17 | convolution fusion | flops 2147745792 | bytes 11010048 | tf_op jit(solution)/shard_map/dot_general | solution.py:90
  254.9 4.9 %all-to-all-start.1 = ((bf16[4,256,256]{1,2,0:T(8,128)(2,1)}), bf16[4,256,256]{1,2,0:T(8,128)(2,1)S(1)}, u32[]{:S(2)}, u32[]{:S(2)}) async-start(bf16[4,256,256]{1,2,0:T(8,128)(2,1)} %bitcast.11), calls=%async_computation.1 | async-start | bytes 1048576 | tf_op jit(solution)/shard_map/all_to_all | solution.py:34
  259.7 0.0 copy-start.4
  259.7 0.0 reduce-scatter.8.cloned.1.call-start
  259.7 7.3 %fusion.15 = bf16[1024,256]{1,0:T(8,128)(2,1)} fusion(bf16[2,256,4096]{2,1,0:T(8,128)(2,1)} %param.11, bf16[2,1024,4096]{2,1,0:T(8,128)(2,1)} %all-gather.2.cloned.1.call-done), kind=kOutput, calls=%fused_computation.18 | convolution fusion | flops 2147745792 | bytes 11010048 | tf_op jit(solution)/shard_map/dot_general | solution.py:90
  267.1 12.1 %reduce-scatter.6.cloned.1.call-done = bf16[2,2,32,4096]{3,2,1,0:T(8,128)(2,1)} async-done(((bf16[8,2,32,4096]{3,2,1,0:T(8,128)(2,1)}), bf16[2,2,32,4096]{3,2,1,0:T(8,128)(2,1)}) %reduce-scatter.6.cloned.1.call-update) | async-done | bytes 1048592 | tf_op jit(solution)/shard_map/reduce_scatter | solution.py:43
  279.1 0.0 reduce-scatter.8.cloned.1.call-update
  279.2 0.0 copy-done.4
  279.2 7.2 %fusion.6 = bf16[1,256,4096]{1,2,0:T(8,128)(2,1)} fusion(bf16[2,1024,4096]{2,1,0:T(8,128)(2,1)} %all-gather.2.cloned.1.call-done, bf16[2,256,1024]{2,1,0:T(8,128)(2,1)S(1)} %copy-done.4), kind=kOutput, calls=%fused_computation.9 | convolution fusion | flops 2148532224 | bytes 11010048 | tf_op jit(solution)/shard_map/dot_general | solution.py:97
  286.4 7.2 %fusion.7 = bf16[1,256,4096]{1,2,0:T(8,128)(2,1)} fusion(bf16[2,1024,4096]{2,1,0:T(8,128)(2,1)} %all-gather.2.cloned.1.call-done, bf16[2,256,1024]{2,1,0:T(8,128)(2,1)S(1)} %copy-done.4), kind=kOutput, calls=%fused_computation.10 | convolution fusion | flops 2148532224 | bytes 11010048 | tf_op jit(solution)/shard_map/dot_general | solution.py:97
  293.6 0.0 all-to-all-done.1
  293.6 5.0 %all-to-all-start = ((bf16[4,256,256]{1,2,0:T(8,128)(2,1)}), bf16[4,256,256]{1,2,0:T(8,128)(2,1)S(1)}, u32[]{:S(2)}, u32[]{:S(2)}) async-start(bf16[4,256,256]{1,2,0:T(8,128)(2,1)} %bitcast.79), calls=%async_computation | async-start | bytes 1048576 | tf_op jit(solution)/shard_map/all_to_all | solution.py:34
  298.7 4.6 %pad_maximum_fusion = bf16[2,256,4096]{1,2,0:T(8,128)(2,1)} fusion(bf16[1,256,4096]{1,2,0:T(8,128)(2,1)} %fusion.7, bf16[1,256,4096]{1,2,0:T(8,128)(2,1)} %fusion.6), kind=kLoop, calls=%fused_computation.11 | loop fusion | flops 2097152 | bytes 8388608 | tf_op jit(solution)/shard_map/stack | solution.py:113
  303.2 4.0 %reduce-scatter.8.cloned.1.call-done = bf16[1,2,32,4096]{3,2,1,0:T(8,128)(2,1)} async-done(((bf16[2,2,32,4096]{3,2,1,0:T(8,128)(2,1)}), bf16[1,2,32,4096]{3,2,1,0:T(8,128)(2,1)}) %reduce-scatter.8.cloned.1.call-update) | async-done | bytes 524304 | tf_op jit(solution)/shard_map/reduce_scatter | solution.py:43
  307.2 1.9 multiply_reduce_fusion
  309.1 0.0 copy-start.1
  309.1 6.4 %copy.22 = bf16[2,256,4096]{2,1,0:T(8,128)(2,1)} copy(bf16[2,256,4096]{1,2,0:T(8,128)(2,1)} %pad_maximum_fusion) | data formatting | bytes 8388608
  315.5 9.1 %psum.35 = f32[]{:T(128)} all-reduce(f32[]{:T(128)} %multiply_reduce_fusion), channel_id=1, replica_groups=mesh['fsdp_0'=4,'fsdp_1'=2,'fsdp_2'=4,'red_0'=2,'red_1'=2] {'fsdp_0'}, use_global_device_ids=true, to_apply=%region_6.7 | all-reduce | flops 1 | bytes 8 | tf_op jit(solution)/shard_map/psum | solution.py:53
  324.6 0.1 reduce_sum.34
  324.6 5.9 %psum.36 = f32[]{:T(128)} all-reduce(f32[]{:T(128)} %psum.35), channel_id=1, replica_groups=mesh['fsdp_0'=4,'fsdp_1'=2,'fsdp_2'=4,'red_0'=2,'red_1'=2] {'fsdp_1'}, use_global_device_ids=true, to_apply=%region_7.8 | all-reduce | flops 1 | bytes 8 | tf_op jit(solution)/shard_map/psum | solution.py:53
  330.6 0.0 all-to-all-done
  330.6 0.1 reduce_sum.33
  330.6 11.5 %psum.37 = f32[]{:T(128)} all-reduce(f32[]{:T(128)} %psum.36), channel_id=1, replica_groups=mesh['fsdp_0'=4,'fsdp_1'=2,'fsdp_2'=4,'red_0'=2,'red_1'=2] {'fsdp_2'}, use_global_device_ids=true, to_apply=%region_8.9 | all-reduce | flops 1 | bytes 8 | tf_op jit(solution)/shard_map/psum | solution.py:53
  342.2 4.4 %psum.38 = f32[]{:T(128)} all-reduce(f32[]{:T(128)} %psum.37), channel_id=1, replica_groups=mesh['fsdp_0'=4,'fsdp_1'=2,'fsdp_2'=4,'red_0'=2,'red_1'=2] {'red_0'}, use_global_device_ids=true, to_apply=%region_9.10 | all-reduce | flops 1 | bytes 8 | tf_op jit(solution)/shard_map/psum | solution.py:53
  346.6 0.8 copy.21
  347.4 10.6 %psum.39 = f32[]{:T(128)} all-reduce(f32[]{:T(128)} %psum.38), channel_id=1, replica_groups=mesh['fsdp_0'=4,'fsdp_1'=2,'fsdp_2'=4,'red_0'=2,'red_1'=2] {'red_1'}, use_global_device_ids=true, to_apply=%region_10.11 | all-reduce | flops 1 | bytes 8 | tf_op jit(solution)/shard_map/psum | solution.py:53
  358.7 0.0 collective-permute-done.1
  358.7 0.0 collective-permute-done.3
  358.7 0.0 copy-done.1
  358.7 4.2 %multiply_subtract_fusion = (f32[2,32,4096]{2,1,0:T(8,128)}, f32[2,32,4096]{2,1,0:T(8,128)}, f32[2,32,4096]{2,1,0:T(8,128)}) fusion(f32[2,32,4096]{2,1,0:T(8,128)S(1)} %copy-done, bf16[2,32,4096]{2,1,0:T(8,128)(2,1)S(1)} %collective-permute-done, pred[]{:T(512)} %eq.3, f32[]{:T(128)S(6)} %min_shard_map.3, f32[]{:T(128)} %bitcast.25, ...), kind=kLoop, calls=%fused_computation.22 | loop fusion | flops 5767168 | bytes 8388617 | tf_op jit(solution)/shard_map/sub | solution.py:110
  (1 shorter events, 0.0 us)
Async XLA Ops:
  8.0 217.5 %reduce-scatter.4.cloned.1.call-start = ((), (), s32[]{:S(2)}) async-start(), calls=%async_computation.6 | async-start | bytes 20971520 | tf_op jit(solution)/shard_map/reduce_scatter | solution.py:43
  34.8 1.2 copy-start.2
  34.8 10.1 %copy-start = (f32[2,32,4096]{2,1,0:T(8,128)S(1)}, f32[2,32,4096]{2,1,0:T(8,128)}, u32[]{:S(2)}) copy-start(f32[2,32,4096]{2,1,0:T(8,128)} %param.14) | copy-start | bytes 3145732
  34.9 212.7 %all-gather.2.cloned.1.call-start = ((), (), s32[]{:S(2)}) async-start(), calls=%async_computation.5 | async-start | bytes 17301504 | tf_op jit(solution)/shard_map/all_gather | solution.py:83
  36.1 8.8 %collective-permute-start = (bf16[2,32,4096]{2,1,0:T(8,128)(2,1)S(1)}, bf16[2,32,4096]{2,1,0:T(8,128)(2,1)S(1)}, u32[]{:S(2)}, u32[]{:S(2)}) collective-permute-start(bf16[2,32,4096]{2,1,0:T(8,128)(2,1)S(1)} %convert_element_type.62), channel_id=1, source_target_pairs={{0,1},{1,2},{2,3},{3,0},{4,5},{5,6},{6,7},{7,4},{8,9},{9,10},{10,1... | collective-permute-start | bytes 1572872 | tf_op jit(solution)/shard_map/ppermute | solution.py:24
  39.4 191.9 %copy-start.3 = (f32[2,32,4096]{2,1,0:T(8,128)S(1)}, f32[2,32,4096]{2,1,0:T(8,128)}, u32[]{:S(2)}) copy-start(f32[2,32,4096]{2,1,0:T(8,128)} %param.20) | copy-start | bytes 3145732
  45.8 233.3 %reduce-scatter.6.cloned.1.call-start = ((), (), s32[]{:S(2)}) async-start(), calls=%async_computation.7 | async-start | bytes 5242880 | tf_op jit(solution)/shard_map/reduce_scatter | solution.py:43
  226.2 7.2 %collective-permute-start.2 = (bf16[1,1]{1,0:T(2,128)(2,1)}, bf16[1,1]{1,0:T(2,128)(2,1)}, u32[]{:S(2)}, u32[]{:S(2)}) collective-permute-start(bf16[1,1]{1,0:T(2,128)(2,1)} %convert_element_type.77), channel_id=1, source_target_pairs={{0,1},{1,2},{2,3},{3,0},{4,5},{5,6},{6,7},{7,4},{8,9},{9,10},{10,1... | collective-permute-start | bytes 14 | tf_op jit(solution)/shard_map/ppermute | solution.py:24
  231.2 127.5 %collective-permute-start.1 = (bf16[2,32,4096]{2,1,0:T(8,128)(2,1)}, bf16[2,32,4096]{2,1,0:T(8,128)(2,1)}, u32[]{:S(2)}, u32[]{:S(2)}) collective-permute-start(bf16[2,32,4096]{2,1,0:T(8,128)(2,1)} %convert_element_type.73), channel_id=1, source_target_pairs={{0,1},{1,2},{2,3},{3,0},{4,5},{5,6},{6,7},{7,4},{8,9},{9,10},{10,1... | collective-permute-start | bytes 1572872 | tf_op jit(solution)/shard_map/ppermute | solution.py:24
  232.1 126.6 %collective-permute-start.3 = (bf16[2,32,4096]{2,1,0:T(8,128)(2,1)}, bf16[2,32,4096]{2,1,0:T(8,128)(2,1)}, u32[]{:S(2)}, u32[]{:S(2)}) collective-permute-start(bf16[2,32,4096]{2,1,0:T(8,128)(2,1)} %convert_element_type.79), channel_id=1, source_target_pairs={{0,1},{1,2},{2,3},{3,0},{4,5},{5,6},{6,7},{7,4},{8,9},{9,10},{10,1... | collective-permute-start | bytes 1572872 | tf_op jit(solution)/shard_map/ppermute | solution.py:24
  254.9 38.8 %all-to-all-start.1 = ((bf16[4,256,256]{1,2,0:T(8,128)(2,1)}), bf16[4,256,256]{1,2,0:T(8,128)(2,1)S(1)}, u32[]{:S(2)}, u32[]{:S(2)}) async-start(bf16[4,256,256]{1,2,0:T(8,128)(2,1)} %bitcast.11), calls=%async_computation.1 | async-start | bytes 1048576 | tf_op jit(solution)/shard_map/all_to_all | solution.py:34
  259.7 19.4 %copy-start.4 = (bf16[2,256,1024]{2,1,0:T(8,128)(2,1)S(1)}, bf16[2,256,1024]{2,1,0:T(8,128)(2,1)}, u32[]{:S(2)}) copy-start(bf16[2,256,1024]{2,1,0:T(8,128)(2,1)} %param.12) | copy-start | bytes 3145732
  259.7 47.5 %reduce-scatter.8.cloned.1.call-start = ((), (), s32[]{:S(2)}) async-start(), calls=%async_computation.8 | async-start | bytes 1572864 | tf_op jit(solution)/shard_map/reduce_scatter | solution.py:43
  293.6 36.9 %all-to-all-start = ((bf16[4,256,256]{1,2,0:T(8,128)(2,1)}), bf16[4,256,256]{1,2,0:T(8,128)(2,1)S(1)}, u32[]{:S(2)}, u32[]{:S(2)}) async-start(bf16[4,256,256]{1,2,0:T(8,128)(2,1)} %bitcast.79), calls=%async_computation | async-start | bytes 1048576 | tf_op jit(solution)/shard_map/all_to_all | solution.py:34
  309.1 49.6 %copy-start.1 = (bf16[1,2,32,4096]{3,2,1,0:T(8,128)(2,1)S(1)}, bf16[1,2,32,4096]{3,2,1,0:T(8,128)(2,1)}, u32[]{:S(2)}) copy-start(bf16[1,2,32,4096]{3,2,1,0:T(8,128)(2,1)} %reduce-scatter.8.cloned.1.call-done) | copy-start | bytes 1572868
Sparse Core Ops, SparseCore 0:
  35.0 190.4 reduce-scatter.3
  227.9 51.1 reduce-scatter.5
  281.5 25.6 reduce-scatter.7
Sparse Core Ops, SparseCore 1:
  45.9 201.7 all-gather.1
where the time goes:
time: 371 us; the launch traced here: 370 us
  waiting for transfers between devices  215 us (58%)
  matrix products  41.8 us (11%)
  blocking collectives  41.5 us (11%)
  local copies, waits for them, and re-layouts  22.4 us (6%)
  between operations  18.5 us (5%)
  starting transfers between devices  16.3 us (4%)
  other arithmetic  14.7 us (4%)
    reduce_scatter x3, waiting for transfers between devices, reduced_to_own(): parts = lax.psum_scatter(parts, axes[k], scatter_dimension=0, tiled=True)  196 us
    psum x5, blocking collectives, by_axis(): return functools.reduce(lax.psum, axes, shard)  41.5 us
    dot_general x2, matrix products, local(): lax.dot_general(inputs, full_weight, (((1,), (1,)), ((), ())), preferred_...  14.6 us
    dot_general x2, matrix products, local(): jnp.dot(upstream, full_weight, preferred_element_type=jnp.float32)  14.5 us
    reshape x1, local copies, waits for them, and re-layouts, reduced_to_own(): parts = parts.reshape(*(lax.axis_size(a) for a in axes), *inside)  14 us
    all_gather x1, waiting for transfers between devices, local(): gathered = lax.all_gather(weights, FSDP, axis=1, tiled=True)  13.6 us
    dot_general x1, matrix products, local(): jnp.einsum('ltc,ltd->lcd', kv_cotangent, layer_input, preferred_element_t...  12.8 us
    all_to_all x2, starting transfers between devices, sent_and_summed(): lax.all_to_all(cut_along(shard, dim, length), axis, 0, 0, tiled=True)  9.91 us
  transfers between devices with their start and end apart: 10, of which 5 were waited for; matrix products, arithmetic and copies ran while one was open for 13% of the time, Pallas kernels for 0%

commit v1 on v0

v1 whole, which is shorter than its diff:
```python
import functools

import jax
import jax.numpy as jnp
from jax import lax
from jax.experimental import pallas as pl
from jax.experimental.pallas import tpu as pltpu
from jax.sharding import Mesh
from jax.sharding import PartitionSpec as P

Y, XH, Z, XL, CO = "fsdp_0", "fsdp_1", "fsdp_2", "red_0", "red_1"
RED = (XL, CO)
FSDP = (Y, XH, Z)
MESH_ID = pl.DeviceIdType.MESH

BETA_FIRST = 0.9
BETA_SECOND = 0.95
LEARN_RATE = 0.01
DECAY_RATE = 0.1
ADAM_EPS = 1e-08
MEAN_EPS = 1e-06

NK = 4
BF = jnp.bfloat16
F32 = jnp.float32


def kernel(
    entries,
    x_in,
    u_in,
    failed,
    scale_own,
    scale_spare,
    master,
    first,
    second,
    sp_master,
    sp_first,
    sp_second,
    kv_out,
    ig_out,
    nm_out,
    nf_out,
    ns_out,
    xbuf,
    ubuf,
    ut,
    wsb,
    wbuf,
    dwbuf,
    r1a,
    r1b,
    r1c,
    s1,
    r2a,
    r2b,
    r2c,
    s2,
    gbuf,
    igb,
    kvp,
    kvs,
    kvr,
    ka,
    kb,
    kc,
    kvo,
    st,
    spf,
    spb,
    spr,
    scs,
    scr,
    nacc,
    nsend,
    npl,
    nsend2,
    nxc,
    loc,
    sp_s,
    sp_r,
    u_s,
    u_r,
    x_s,
    x_r,
    w_s,
    w_r,
    ag_s,
    ag_r,
    rs_s,
    rs_r,
    g_s,
    g_r,
    ig_s,
    ig_r,
    kv_s,
    kv_r,
    np_s,
    np_r,
    nx_s,
    nx_r,
):
    layers, tok, cols = x_in.shape
    half = cols // 2
    ck = half // NK
    rows = master.shape[1]
    feats = u_in.shape[2]
    y, xh, z, xl, c = (lax.axis_index(a) for a in (Y, XH, Z, XL, CO))
    x = 2 * xh + xl
    me_r = 2 * xl + c

    def ring(v, d):
        return lax.rem(v + (d + 4), 4)

    def to_x(v, core=None):
        dev = {XH: v // 2, XL: lax.rem(v, 2)}
        if core is not None:
            dev[CO] = core
        return dev

    xn = {d: ring(x, d) for d in (1, -1)}
    xn_h = {d: xn[d] // 2 for d in (1, -1)}
    plane_axis = {0: (Y, Z), 1: (Z, Y)}
    plane_pos = {Y: y, Z: z}
    DIRS = ((0, 1), (1, -1))

    def remote(src, dst, ss, rs, dev):
        return pltpu.make_async_remote_copy(
            src_ref=src, dst_ref=dst, send_sem=ss, recv_sem=rs, device_id=dev, device_id_type=MESH_ID
        )

    sends = []

    states = (master, first, second)
    spares = (sp_master, sp_first, sp_second)
    loads_sp = [pltpu.make_async_copy(spares[i], spf.at[i], loc.at[i]) for i in range(3)]
    loads_st = [pltpu.make_async_copy(states[i], st.at[i], loc.at[3 + i]) for i in range(3)]
    load_u = pltpu.make_async_copy(u_in, ubuf.at[:, xh], loc.at[6])
    loads_sp[0].start()
    loads_st[0].start()
    load_u.start()
    loads_sp[1].start()
    loads_sp[2].start()
    loads_st[1].start()
    loads_st[2].start()

    nxt_r = lax.rem(me_r + 1, 4)
    prv_r = lax.rem(me_r + 3, 4)
    plane_peers = [(dy, dz) for dy in range(4) for dz in range(4) if (dy, dz) != (0, 0)]
    xc_peers = [(dx, dc) for dx in range(4) for dc in range(2) if (dx, dc) != (0, 0)]

    def plane_dev(dy, dz):
        return {Y: lax.rem(y + dy, 4), Z: lax.rem(z + dz, 4)}

    def xc_dev(dx, dc):
        v = lax.rem(x + dx, 4)
        return {XH: v // 2, XL: lax.rem(v, 2), CO: lax.rem(c + dc, 2)}

    barrier = pltpu.get_barrier_semaphore()
    for p in plane_peers:
        pl.semaphore_signal(barrier, inc=1, device_id=plane_dev(*p), device_id_type=MESH_ID)
    for p in xc_peers:
        pl.semaphore_signal(barrier, inc=1, device_id=xc_dev(*p), device_id_type=MESH_ID)

    loads_sp[0].wait()
    for l in range(layers):
        spb[0, l] = spf[0, l].astype(BF)
    scs[...] = jnp.broadcast_to(scale_spare[...], scs.shape)
    pl.semaphore_wait(barrier, len(plane_peers) + len(xc_peers))

    nxt_dev = {XL: nxt_r // 2, CO: lax.rem(nxt_r, 2)}

    def spare_copy(i, l):
        if i == 0:
            return remote(spb.at[0, l], spr.at[0, l], sp_s.at[l], sp_r.at[l], nxt_dev)
        return remote(spb.at[i], spr.at[i], sp_s.at[1 + i], sp_r.at[1 + i], nxt_dev)

    for l in range(layers):
        spare_copy(0, l).start()
    scale_copy = remote(scs, scr, sp_s.at[4], sp_r.at[4], nxt_dev)
    scale_copy.start()

    def x_copy(k, l, di, d):
        src = x_in.at[l, :, pl.ds(pl.multiple_of(xn_h[d] * half + k * ck, ck), ck)]
        return remote(src, xbuf.at[k, l, xh], x_s.at[k, l, di], x_r.at[k, l, di], to_x(xn[d]))

    for di, d in DIRS:
        x_copy(0, 0, di, d).start()

    def w_copy(l, di, d):
        return remote(
            wsb.at[xn_h[d], :, l], wbuf.at[:, l, y, xh, z], w_s.at[l, di], w_r.at[l, di], to_x(xn[d])
        )

    lost = jnp.broadcast_to(failed[...], (rows, ck)) == me_r
    loads_st[0].wait()
    for l in range(layers):
        spare_copy(0, l).wait_recv()
        for j in range(2 * NK):
            span = slice(j * ck, (j + 1) * ck)
            now = jnp.where(lost, spr[0, l, :, span].astype(F32), st[0, l, :, span])
            st[0, l, :, span] = now
            wsb[j // NK, j % NK, l] = now.astype(BF)
        for di, d in DIRS:
            w_copy(l, di, d).start()

    load_u.wait()
    u_far = lax.rem(x + 1 + 2 * (1 - lax.rem(x, 2)), 4)
    u_copy = remote(u_in.at[c], ubuf.at[c, xh], u_s.at[0], u_r.at[0], to_x(u_far))
    u_copy.start()
    u_fwd = remote(ubuf.at[c, 1 - xh], ubuf.at[c, 1 - xh], u_s.at[1], u_r.at[1], {CO: 1 - c})

    for di, d in DIRS:
        x_copy(0, 1, di, d).start()
    for l in range(layers):
        for di, d in DIRS:
            x_copy(1, l, di, d).start()
    for i in (1, 2):
        loads_sp[i].wait()
        for l in range(layers):
            spb[i, l] = spf[i, l].astype(BF)
        spare_copy(i, 0).start()
    for k in range(2, NK):
        for l in range(layers):
            for di, d in DIRS:
                x_copy(k, l, di, d).start()

    def region(k, l, stage, p, h):
        hs = slice(None) if h is None else h
        if l == 0:
            return wbuf.at[k, 0, p, hs, z] if stage == 0 else wbuf.at[k, 0, :, hs, p]
        return wbuf.at[k, 1, y, hs, p] if stage == 0 else wbuf.at[k, 1, p, hs, :]

    def ag_copy(k, l, stage, step, di, d):
        axis = plane_axis[l][stage]
        pos = plane_pos[axis]
        ref = region(k, l, stage, pos, None) if step == 0 else region(k, l, stage, ring(pos, -d), di)
        n = stage * 2 + step
        return remote(ref, ref, ag_s.at[k, l, n, di], ag_r.at[k, l, n, di], {axis: ring(pos, d)})

    def ag_start(k, stage):
        for l in range(layers):
            for di, d in DIRS:
                ag_copy(k, l, stage, 0, di, d).start()

    def ag_forward(k, stage):
        for l in range(layers):
            for di, d in DIRS:
                ag_copy(k, l, stage, 0, di, d).wait_recv()
                ag_copy(k, l, stage, 1, di, d).start()

    def ag_finish(k, stage):
        for l in range(layers):
            for di, d in DIRS:
                ag_copy(k, l, stage, 1, di, d).wait_recv()

    def dw_piece(k, l, p, h):
        return dwbuf.at[k, 0, :, h, p] if l == 0 else dwbuf.at[k, 1, p, h, :]

    def rs_parts(k, l, stage):
        axis = plane_axis[l][1 - stage]
        if stage == 0:
            return axis, (lambda p, h: dw_piece(k, l, p, h)), r1a, r1b, r1c
        return axis, (lambda p, h: s1.at[k, l, h, p]), r2a, r2b, r2c

    def rs_copy(k, l, stage, what, di, d):
        axis, piece, ra, rb, rc = rs_parts(k, l, stage)
        pos = plane_pos[axis]
        if what == 0:
            src, dst = piece(ring(pos, 2), di), ra.at[k, l, di]
        elif what == 1:
            src, dst = piece(ring(pos, d), 1 - di), rb.at[k, l, di]
        else:
            src, dst = ra.at[k, l, di], rc.at[k, l, di]
        n = stage * 3 + what
        return remote(src, dst, rs_s.at[k, l, n, di], rs_r.at[k, l, n, di], {axis: ring(pos, d)})

    def rs_start(k, l, stage):
        for what in (0, 1):
            for di, d in DIRS:
                rs_copy(k, l, stage, what, di, d).start()

    def each(stage, fn):
        if stage == 0:

            @pl.loop(0, 4)
            def _(j):
                fn(j)
        else:
            fn(None)

    def at(ref, j):
        return ref[j] if j is not None else ref[...]

    def rs_forward(k, stage):
        for l in range(layers):
            axis, piece, ra, rb, rc = rs_parts(k, l, stage)
            pos = plane_pos[axis]
            for di, d in DIRS:
                rs_copy(k, l, stage, 0, di, d).wait_recv()
                own = piece(ring(pos, d), di)
                acc = ra.at[k, l, di]

                def add(j, own=own, acc=acc):
                    total = (at(acc, j).astype(F32) + at(own, j).astype(F32)).astype(BF)
                    if j is None:
                        acc[...] = total
                    else:
                        acc[j] = total

                each(stage, add)
                rs_copy(k, l, stage, 2, di, d).start()

    def rs_finish(k, stage):
        for l in range(layers):
            axis, piece, ra, rb, rc = rs_parts(k, l, stage)
            pos = plane_pos[axis]
            for what in (1, 2):
                for di, d in DIRS:
                    rs_copy(k, l, stage, what, di, d).wait_recv()
            for h in range(2):
                own = piece(pos, h)
                through = rc.at[k, l, h]
                direct = rb.at[k, l, 1 - h]
                out = s1.at[k, l, h] if stage == 0 else s2.at[k, l, h]

                def add(j, own=own, through=through, direct=direct, out=out):
                    total = at(own, j).astype(F32) + at(through, j).astype(F32) + at(direct, j).astype(F32)
                    if j is None:
                        out[...] = total.astype(BF)
                    else:
                        out[j] = total.astype(BF)

                each(stage, add)
            if stage == 0:
                rs_start(k, l, 1)
            else:
                for di, d in DIRS:
                    g_copy(k, l, di, d).start()

    def g_copy(k, l, di, d):
        return remote(
            s2.at[k, l, xn_h[d]], gbuf.at[k, l, xh], g_s.at[k, l, di], g_r.at[k, l, di], to_x(xn[d])
        )

    def transpose_u():
        for l in range(layers):

            @pl.loop(0, 4)
            def _(j):
                span = pl.ds(pl.multiple_of(j * (feats // 4), feats // 4), feats // 4)
                for t in range(2):
                    ut[l, j, :, t * tok : (t + 1) * tok] = ubuf[l, t, :, span].T

    def grad_product(k):
        for l in range(layers):
            for di, d in DIRS:
                x_copy(k, l, di, d).wait_recv()

            @pl.loop(0, 4)
            def _(j):
                inputs = xbuf[k, l].reshape(2 * tok, ck)
                part = jnp.dot(ut[l, j], inputs, preferred_element_type=F32)
                dwbuf[k, l, j] = part.astype(BF).reshape(2, 4, rows, ck)

            rs_start(k, l, 0)

    def weight_products(k, begin):
        for l in range(layers):

            @pl.loop(0, 4)
            def _(j):
                inputs = xbuf[k, l].reshape(2 * tok, ck)
                weight = wbuf[k, l, j].reshape(8 * rows, ck)
                part = lax.dot_general(
                    inputs, weight, (((1,), (1,)), ((), ())), preferred_element_type=F32
                ).reshape(2, tok, 8 * rows)
                if begin is True:
                    kvp[j, l] = part
                else:
                    kvp[j, l] += part

            @pl.loop(0, 2)
            def _(t):
                weight = wbuf[k, l].reshape(feats, ck)
                igb[k, l, t] = jnp.dot(ubuf[l, t], weight, preferred_element_type=F32).astype(BF)

            for di, d in DIRS:
                ig_copy(k, l, di, d).start()

    def ig_copy(k, l, di, d):
        dst = ig_out.at[l, :, pl.ds(pl.multiple_of(xh * half + k * ck, ck), ck)]
        return remote(igb.at[k, l, xn_h[d]], dst, ig_s.at[k, l, di], ig_r.at[k, l, di], to_x(xn[d]))

    for l in range(layers):
        for di, d in DIRS:
            w_copy(l, di, d).wait_recv()
    for k in range(NK):
        ag_start(k, 0)

    @pl.loop(0, 4)
    def _(j):
        kvp[j] = jnp.zeros(kvp.shape[1:], F32)

    u_copy.wait_recv()
    u_fwd.start()
    ag_forward(0, 0)
    u_fwd.wait_recv()
    transpose_u()

    @pl.loop(0, NK)
    def _(i):
        @pl.when(i > 0)
        def _():
            ag_forward(i, 0)
            rs_forward(i - 1, 0)

        ag_finish(i, 0)
        ag_start(i, 1)
        grad_product(i)

        @pl.when(i > 0)
        def _():
            rs_finish(i - 1, 0)

        ag_forward(i, 1)

        @pl.when(i > 0)
        def _():
            weight_products(i - 1, False)
            rs_forward(i - 1, 1)

        ag_finish(i, 1)

        @pl.when(i > 0)
        def _():
            rs_finish(i - 1, 1)

    last = NK - 1
    rs_forward(last, 0)
    weight_products(last, False)

    for v in range(2):
        kvs[v] = kvp[2 * v + (1 - c)].astype(BF)
    kv_core = remote(kvs, kvr, kv_s.at[0], kv_r.at[0], {CO: 1 - c})
    kv_core.start()
    rs_finish(last, 0)
    kv_core.wait_recv()
    for v in range(2):
        for l in range(layers):
            kvr[v, l] = (kvr[v, l].astype(F32) + kvp[2 * v + c, l]).astype(BF)

    def kv_piece(v, l):
        return kvr.at[lax.rem(v, 2), l, v // 2]

    def kv_copy(what, di, d):
        if what == 0:
            src, dst = kv_piece(ring(x, 2), di), ka.at[di]
        elif what == 1:
            src, dst = kv_piece(ring(x, d), 1 - di), kb.at[di]
        else:
            src, dst = ka.at[di], kc.at[di]
        n = 1 + what * 2 + di
        return remote(src, dst, kv_s.at[n], kv_r.at[n], to_x(xn[d]))

    for what in (0, 1):
        for di, d in DIRS:
            kv_copy(what, di, d).start()
    rs_forward(last, 1)
    for di, d in DIRS:
        kv_copy(0, di, d).wait_recv()
        ka[di] = (ka[di].astype(F32) + kv_piece(ring(x, d), di)[...].astype(F32)).astype(BF)
        kv_copy(2, di, d).start()
    rs_finish(last, 1)

    scale_copy.wait_recv()
    lost_tile = jnp.broadcast_to(failed[...], scr.shape) == me_r
    scr[...] = jnp.where(lost_tile, scr[...], jnp.broadcast_to(scale_own[...], scr.shape))
    scale = jnp.broadcast_to(scr[0:1, 0:1], (rows, ck))
    nacc[...] = jnp.zeros(nacc.shape, F32)
    for k in range(NK):
        for l in range(layers):
            for di, d in DIRS:
                g_copy(k, l, di, d).wait_recv()

    @pl.loop(0, NK)
    def _(k):
        for l in range(layers):
            for h in range(2):
                grad = gbuf[k, l, h].astype(F32) / scale
                nacc[...] += grad * grad

    tile = jnp.zeros((8, 128), F32)
    for i in range(rows // 8):
        for j in range(ck // 128):
            tile = tile + nacc[8 * i : 8 * i + 8, 128 * j : 128 * j + 128]
    nsend[...] = tile
    np_copies = [
        remote(nsend, npl.at[i], np_s.at[i], np_r.at[i], plane_dev(*p)) for i, p in enumerate(plane_peers)
    ]
    for cp in np_copies:
        cp.start()
    for what in (1, 2):
        for di, d in DIRS:
            kv_copy(what, di, d).wait_recv()
    for h in range(2):
        own = kv_piece(x, h)[...].astype(F32)
        kvo[h] = (own + kc[h].astype(F32) + kb[1 - h].astype(F32)).astype(BF)
    kv_store = pltpu.make_async_copy(kvo, kv_out, loc.at[7])
    kv_store.start()
    total = nsend[...]
    for i, cp in enumerate(np_copies):
        cp.wait_recv()
        total = total + npl[i]
    nsend2[...] = total
    nx_copies = [
        remote(nsend2, nxc.at[i], nx_s.at[i], nx_r.at[i], xc_dev(*p)) for i, p in enumerate(xc_peers)
    ]
    for cp in nx_copies:
        cp.start()
    for i in (1, 2):
        loads_st[i].wait()
        spare_copy(i, 0).wait_recv()
    total = nsend2[...]
    for i, cp in enumerate(nx_copies):
        cp.wait_recv()
        total = total + nxc[i]
    squares = jnp.sum(jnp.sum(total, axis=1, keepdims=True), axis=0, keepdims=True)
    factor = jnp.minimum(1.0, lax.rsqrt(squares / entries + MEAN_EPS))
    factor = jnp.broadcast_to(factor, (rows, ck))

    @pl.loop(0, 2 * NK)
    def _(j):
        span = pl.ds(pl.multiple_of(j * ck, ck), ck)
        h = j // NK
        k = lax.rem(j, NK)
        for l in range(layers):
            clipped = gbuf[k, l, h].astype(F32) / scale * factor
            first_now = jnp.where(lost, spr[1, l, :, span].astype(F32), st[1, l, :, span])
            second_now = jnp.where(lost, spr[2, l, :, span].astype(F32), st[2, l, :, span])
            master_now = st[0, l, :, span]
            new_first = BETA_FIRST * first_now + (1.0 - BETA_FIRST) * clipped
            new_second = BETA_SECOND * second_now + (1.0 - BETA_SECOND) * clipped * clipped
            st[0, l, :, span] = master_now - LEARN_RATE * (
                new_first / (jnp.sqrt(new_second) + ADAM_EPS) + DECAY_RATE * master_now
            )
            st[1, l, :, span] = new_first
            st[2, l, :, span] = new_second

    stores = [
        pltpu.make_async_copy(st.at[i], out, loc.at[8 + i]) for i, out in enumerate((nm_out, nf_out, ns_out))
    ]
    for cp in stores:
        cp.start()

    for l in range(layers):
        spare_copy(0, l).wait_send()
    for i in (1, 2):
        spare_copy(i, 0).wait_send()
    scale_copy.wait_send()
    u_copy.wait_send()
    u_fwd.wait_send()
    kv_core.wait_send()
    for l in range(layers):
        for di, d in DIRS:
            w_copy(l, di, d).wait_send()
    for what in range(3):
        for di, d in DIRS:
            kv_copy(what, di, d).wait_send()
    for cp in np_copies + nx_copies:
        cp.wait_send()

    @pl.loop(0, NK)
    def _(k):
        for l in range(layers):
            for di, d in DIRS:
                x_copy(k, l, di, d).wait_send()
                ig_copy(k, l, di, d).wait_send()
                g_copy(k, l, di, d).wait_send()
                for stage in range(2):
                    for step in range(2):
                        ag_copy(k, l, stage, step, di, d).wait_send()
                    for what in range(3):
                        rs_copy(k, l, stage, what, di, d).wait_send()
                ig_copy(k, l, di, d).wait_recv()

    kv_store.wait()
    for cp in stores:
        cp.wait()


def local(
    layer_input,
    kv_cotangent,
    failed_member,
    master,
    first_moment,
    second_moment,
    loss_scale,
    spare_master,
    spare_first,
    spare_second,
    spare_scale,
):
    layers, tok, cols = layer_input.shape
    rows = master.shape[1]
    feats = kv_cotangent.shape[2]
    half = cols // 2
    ck = half // NK
    entries = float(layers * rows * lax.axis_size(FSDP) * cols * lax.axis_size(RED))
    any_ = pl.BlockSpec(memory_space=pl.ANY)
    vmem = pl.BlockSpec(memory_space=pltpu.VMEM)
    sem = pltpu.SemaphoreType.DMA
    scratch = [
        pltpu.VMEM((NK, layers, 2, tok, ck), BF),
        pltpu.VMEM((layers, 2, tok, feats), BF),
        pltpu.VMEM((layers, 4, feats // 4, 2 * tok), BF),
        pltpu.VMEM((2, NK, layers, rows, ck), BF),
        pltpu.VMEM((NK, layers, 4, 2, 4, rows, ck), BF),
        pltpu.VMEM((NK, layers, 4, 2, 4, rows, ck), BF),
        pltpu.VMEM((NK, layers, 2, 4, rows, ck), BF),
        pltpu.VMEM((NK, layers, 2, 4, rows, ck), BF),
        pltpu.VMEM((NK, layers, 2, 4, rows, ck), BF),
        pltpu.VMEM((NK, layers, 2, 4, rows, ck), BF),
        pltpu.VMEM((NK, layers, 2, rows, ck), BF),
        pltpu.VMEM((NK, layers, 2, rows, ck), BF),
        pltpu.VMEM((NK, layers, 2, rows, ck), BF),
        pltpu.VMEM((NK, layers, 2, rows, ck), BF),
        pltpu.VMEM((NK, layers, 2, rows, ck), BF),
        pltpu.VMEM((NK, layers, 2, tok, ck), BF),
        pltpu.VMEM((4, layers, 2, tok, feats // 4), F32),
        pltpu.VMEM((2, layers, 2, tok, feats // 4), BF),
        pltpu.VMEM((2, layers, 2, tok, feats // 4), BF),
        pltpu.VMEM((2, tok, feats // 4), BF),
        pltpu.VMEM((2, tok, feats // 4), BF),
        pltpu.VMEM((2, tok, feats // 4), BF),
        pltpu.VMEM((2, tok, feats // 4), BF),
        pltpu.VMEM((3, layers, rows, cols), F32),
        pltpu.VMEM((3, layers, rows, cols), F32),
        pltpu.VMEM((3, layers, rows, cols), BF),
        pltpu.VMEM((3, layers, rows, cols), BF),
        pltpu.VMEM((8, 128), F32),
        pltpu.VMEM((8, 128), F32),
        pltpu.VMEM((rows, ck), F32),
        pltpu.VMEM((8, 128), F32),
        pltpu.VMEM((15, 8, 128), F32),
        pltpu.VMEM((8, 128), F32),
        pltpu.VMEM((7, 8, 128), F32),
        sem((11,)),
        sem((5,)),
        sem((5,)),
        sem((2,)),
        sem((2,)),
        sem((NK, layers, 2)),
        sem((NK, layers, 2)),
        sem((layers, 2)),
        sem((layers, 2)),
        sem((NK, layers, 4, 2)),
        sem((NK, layers, 4, 2)),
        sem((NK, layers, 6, 2)),
        sem((NK, layers, 6, 2)),
        sem((NK, layers, 2)),
        sem((NK, layers, 2)),
        sem((NK, layers, 2)),
        sem((NK, layers, 2)),
        sem((7,)),
        sem((7,)),
        sem((15,)),
        sem((15,)),
        sem((7,)),
        sem((7,)),
    ]
    return pl.pallas_call(
        functools.partial(kernel, entries),
        out_shape=(
            jax.ShapeDtypeStruct((layers, tok, feats // 4), BF),
            jax.ShapeDtypeStruct((layers, tok, cols), BF),
            jax.ShapeDtypeStruct(master.shape, F32),
            jax.ShapeDtypeStruct(master.shape, F32),
            jax.ShapeDtypeStruct(master.shape, F32),
        ),
        in_specs=[any_, any_, vmem, vmem, vmem] + [any_] * 6,
        out_specs=(any_,) * 5,
        scratch_shapes=scratch,
        compiler_params=pltpu.CompilerParams(
            collective_id=0, has_side_effects=True, vmem_limit_bytes=67043328
        ),
        name="restore_step",
    )(
        layer_input,
        kv_cotangent,
        failed_member.reshape(1, 1),
        loss_scale,
        spare_scale,
        master,
        first_moment,
        second_moment,
        spare_master,
        spare_first,
        spare_second,
    )


def solution(mesh):
    split = Mesh(mesh.devices.reshape(4, 2, 4, 2, 2), (Y, XH, Z, XL, CO))
    placed = (
        P(None, FSDP, RED),
        P(None, FSDP, None),
        P(FSDP),
        P(None, FSDP, RED),
        P(None, FSDP, RED),
        P(None, FSDP, RED),
        P(FSDP, RED),
        P(None, FSDP, RED),
        P(None, FSDP, RED),
        P(None, FSDP, RED),
        P(FSDP, RED),
    )
    return jax.shard_map(
        local,
        mesh=split,
        in_specs=placed,
        out_specs=(P(None, FSDP, RED),) * 5,
        check_vma=False,
    )
```

time: 371 us -> 177 us (0.48)
  waiting for transfers between devices: 215 us -> 0 us
  Pallas kernels: 0 us -> 165 us
  matrix products: 41.8 us -> 0 us
  blocking collectives: 41.5 us -> 0 us
  starting transfers between devices: 16.3 us -> 0 us
  between operations: 18.5 us -> 2.59 us
  other arithmetic: 14.7 us -> 0 us
  local copies, waits for them, and re-layouts: 22.4 us -> 9.44 us
    reduce_scatter x3 -> x0, waiting for transfers between devices: 196 us -> none  [reduced_to_own(): parts = lax.psum_scatter(parts, axes[k], scatter_dimension=0, tiled=True)]
    pallas_call x0 -> x1, Pallas kernels: none -> 165 us  [local(): pl.pallas_call(functools.partial(kernel, entries), out_shape=(jax.ShapeDt...]
    dot_general x5 -> x0, matrix products: 41.8 us -> none  [the longest x2 14.6 us: local(): lax.dot_general(inputs, full_weight, (((1,), (1,)), ((), ())), preferred_...]
    psum x5 -> x0, blocking collectives: 41.5 us -> none  [by_axis(): return functools.reduce(lax.psum, axes, shard)]
    reshape x1 -> x0, local copies, waits for them, and re-layouts: 14 us -> none  [reduced_to_own(): parts = parts.reshape(*(lax.axis_size(a) for a in axes), *inside)]
    all_gather x1 -> x0, waiting for transfers between devices: 13.6 us -> none  [local(): gathered = lax.all_gather(weights, FSDP, axis=1, tiled=True)]
    all_to_all x2 -> x0, starting transfers between devices: 9.91 us -> none  [sent_and_summed(): lax.all_to_all(cut_along(shard, dim, length), axis, 0, 0, tiled=True)]
    ppermute x4 -> x0, starting transfers between devices: 6.26 us -> none  [shifted(): lax.ppermute(shard, axis, [(i, (i + by) % length) for i in range(length)])]
  transfers between devices with their start and end apart: 10 -> 0, of which waited for: 5 -> 0; matrix products, arithmetic and copies ran while one was open for 13% -> 0% of each run, Pallas kernels for 0% -> 0%
where the time goes in v1:
time: 177 us
  Pallas kernels  165 us (93%)
  local copies, waits for them, and re-layouts  9.44 us (5%)
  between operations  2.59 us (1%)
    pallas_call x1, Pallas kernels, local(): pl.pallas_call(functools.partial(kernel, entries), out_shape=(jax.ShapeDt...  165 us
    unnamed x11, local copies, waits for them, and re-layouts  9.44 us

profile of v1, /device:TPU:1, one launch (start us, length us, event | category | flops | bytes accessed | tf_op | source)
XLA Modules:
  0.0 176.9 jit_solution(17930574520875124341)
XLA Ops:
  2.6 164.9 %restore_step.1 = (bf16[2,256,256]{2,1,0:T(8,128)(2,1)}, bf16[2,256,4096]{2,1,0:T(8,128)(2,1)}, f32[2,32,4096]{2,1,0:T(8,128)}, f32[2,32,4096]{2,1,0:T(8,128)}, f32[2,32,4096]{2,1,0:T(8,128)}) custom-call(bf16[2,256,4096]{2,1,0:T(8,128)(2,1)} %x_in.1, bf16[2,256,1024]{2,1,0:T(8,128)(2,1)} %u_in.1, s32[1,1]{1,0:T(1,128)} %bitcast.1.failed, ...), custom_call_target="tpu_custom_call" | custom-call | tf_op jit(solution)/shard_map/restore_step/pallas_call | solution.py:674
  167.4 1.7 copy.24
  169.1 0.0 copy-start.2
  169.1 0.0 copy-start.1
  169.1 4.8 %copy.25 = bf16[2,256,4096]{2,1,0:T(8,128)(2,1)} copy(bf16[2,256,4096]{2,1,0:T(8,128)(2,1)} %get-tuple-element.11) | data formatting | bytes 8388608
  174.0 0.0 copy-done.2
  174.0 0.0 copy-start
  174.0 1.0 copy.26
  174.9 0.0 copy-done.1
  174.9 1.0 copy.27
  175.9 0.0 copy-done
  175.9 1.0 copy.28
Async XLA Ops:
  169.1 4.9 %copy-start.2 = (f32[2,32,4096]{2,1,0:T(8,128)S(1)}, f32[2,32,4096]{2,1,0:T(8,128)}, u32[]{:S(2)}) copy-start(f32[2,32,4096]{2,1,0:T(8,128)} %get-tuple-element.12) | copy-start | bytes 3145732
  169.1 5.8 %copy-start.1 = (f32[2,32,4096]{2,1,0:T(8,128)S(1)}, f32[2,32,4096]{2,1,0:T(8,128)}, u32[]{:S(2)}) copy-start(f32[2,32,4096]{2,1,0:T(8,128)} %get-tuple-element.13) | copy-start | bytes 3145732
  174.0 1.9 %copy-start = (f32[2,32,4096]{2,1,0:T(8,128)S(1)}, f32[2,32,4096]{2,1,0:T(8,128)}, u32[]{:S(2)}) copy-start(f32[2,32,4096]{2,1,0:T(8,128)} %get-tuple-element.14) | copy-start | bytes 3145732

commit v2 on v1

v2 whole, which is shorter than its diff:
```python
import functools

import jax
import jax.numpy as jnp
from jax import lax
from jax.experimental import pallas as pl
from jax.experimental.pallas import tpu as pltpu
from jax.sharding import Mesh
from jax.sharding import PartitionSpec as P

Y, XH, Z, XL, CO = "fsdp_0", "fsdp_1", "fsdp_2", "red_0", "red_1"
RED = (XL, CO)
FSDP = (Y, XH, Z)
MESH_ID = pl.DeviceIdType.MESH

BETA_FIRST = 0.9
BETA_SECOND = 0.95
LEARN_RATE = 0.01
DECAY_RATE = 0.1
ADAM_EPS = 1e-08
MEAN_EPS = 1e-06

NK = 4
SPARES_AT = 4
ORDER = (
    ("INI",),
    ("WSEL", 0),
    ("WSEL", 1),
    ("XREST",),
    ("A1", 0, 0),
    ("A1", 1, 0),
    ("A1", 2, 0),
    ("A1", 3, 0),
    ("A1", 0, 1),
    ("A1", 1, 1),
    ("A1", 2, 1),
    ("A1", 3, 1),
    ("F0", 0, 0),
    ("F0", 1, 0),
    ("F0", 2, 0),
    ("F0", 0, 1),
    ("F0", 3, 0),
    ("F0", 1, 1),
    ("S1", 0, 0),
    ("UF",),
    ("S1", 1, 0),
    ("F0", 2, 1),
    ("S1", 2, 0),
    ("S1", 3, 0),
    ("F0", 3, 1),
    ("TR",),
    ("S1", 0, 1),
    ("S1", 1, 1),
    ("DW", 0, 0),
    ("F1", 0, 0),
    ("DW", 0, 1),
    ("F1", 0, 1),
    ("F1", 1, 0),
    ("S1", 2, 1),
    ("DW", 1, 0),
    ("F1", 1, 1),
    ("RF0", 0, 1),
    ("F1", 2, 0),
    ("DW", 1, 1),
    ("WD", 0, 1),
    ("KV", 0, 1),
    ("IG", 0, 1),
    ("S1", 3, 1),
    ("F1", 3, 0),
    ("DW", 2, 0),
    ("RF0", 0, 0),
    ("F1", 2, 1),
    ("WD", 1, 1),
    ("KV", 1, 1),
    ("IG", 1, 1),
    ("WD", 0, 0),
    ("KV", 0, 0),
    ("RE0", 0, 1),
    ("WD", 1, 0),
    ("KV", 1, 0),
    ("RF0", 1, 1),
    ("IG", 0, 0),
    ("RF0", 1, 0),
    ("IG", 1, 0),
    ("DW", 2, 1),
    ("DW", 3, 0),
    ("WD", 2, 0),
    ("KV", 2, 0),
    ("IG", 2, 0),
    ("F1", 3, 1),
    ("WD", 3, 0),
    ("KV", 3, 0),
    ("IG", 3, 0),
    ("WD", 2, 1),
    ("KV", 2, 1),
    ("RF0", 2, 0),
    ("RE0", 1, 1),
    ("IG", 2, 1),
    ("DW", 3, 1),
    ("RF0", 2, 1),
    ("RE0", 0, 0),
    ("RF1", 0, 1),
    ("WD", 3, 1),
    ("KV", 3, 1),
    ("KVC",),
    ("RE0", 1, 0),
    ("RF0", 3, 1),
    ("RF0", 3, 0),
    ("KVA",),
    ("RE0", 2, 1),
    ("RE0", 2, 0),
    ("RF1", 0, 0),
    ("RF1", 1, 1),
    ("RF1", 1, 0),
    ("RE1", 0, 1),
    ("RE0", 3, 0),
    ("RE0", 3, 1),
    ("RF1", 2, 1),
    ("RF1", 2, 0),
    ("RE1", 1, 1),
    ("RE1", 0, 0),
    ("RE1", 1, 0),
    ("RF1", 3, 1),
    ("RF1", 3, 0),
    ("RE1", 2, 1),
    ("RE1", 2, 0),
    ("RE1", 3, 1),
    ("RE1", 3, 0),
    ("SQ",),
    ("NX",),
    ("IG", 3, 1),
    ("KVF",),
    ("AD",),
    ("END",),
    ("KVE",),
)
BF = jnp.bfloat16
F32 = jnp.float32


def kernel(
    entries,
    x_in,
    u_in,
    failed,
    scale_own,
    scale_spare,
    master,
    first,
    second,
    sp_master,
    sp_first,
    sp_second,
    kv_out,
    ig_out,
    nm_out,
    nf_out,
    ns_out,
    xbuf,
    ubuf,
    ut,
    wsb,
    wbuf,
    dwbuf,
    r1a,
    r1b,
    r1c,
    s1,
    r2a,
    r2b,
    r2c,
    s2,
    gbuf,
    igb,
    kvp,
    kvs,
    kvr,
    ka,
    kb,
    kc,
    kvo,
    st,
    spf,
    spb,
    spr,
    scs,
    scr,
    scn,
    nacc,
    nsend,
    npl,
    nsend2,
    nxc,
    loc,
    sp_s,
    sp_r,
    u_s,
    u_r,
    x_s,
    x_r,
    w_s,
    w_r,
    ag_s,
    ag_r,
    rs_s,
    rs_r,
    g_s,
    g_r,
    ig_s,
    ig_r,
    kv_s,
    kv_r,
    np_s,
    np_r,
    nx_s,
    nx_r,
    sc_s,
    sc_r,
):
    layers, tok, cols = x_in.shape
    half = cols // 2
    ck = half // NK
    rows = master.shape[1]
    feats = u_in.shape[2]
    y, xh, z, xl, c = (lax.axis_index(a) for a in (Y, XH, Z, XL, CO))
    x = 2 * xh + xl
    me_r = 2 * xl + c

    def ring(v, d):
        return lax.rem(v + (d + 4), 4)

    def to_x(v, core=None):
        dev = {XH: v // 2, XL: lax.rem(v, 2)}
        if core is not None:
            dev[CO] = core
        return dev

    xn = {d: ring(x, d) for d in (1, -1)}
    xn_h = {d: xn[d] // 2 for d in (1, -1)}
    plane_axis = {0: (Y, Z), 1: (Z, Y)}
    plane_pos = {Y: y, Z: z}
    DIRS = ((0, 1), (1, -1))

    def remote(src, dst, ss, rs, dev):
        return pltpu.make_async_remote_copy(
            src_ref=src, dst_ref=dst, send_sem=ss, recv_sem=rs, device_id=dev, device_id_type=MESH_ID
        )

    states = (master, first, second)
    spares = (sp_master, sp_first, sp_second)
    loads_sp = [pltpu.make_async_copy(spares[i], spf.at[i], loc.at[i]) for i in range(3)]
    loads_st = [pltpu.make_async_copy(states[i], st.at[i], loc.at[3 + i]) for i in range(3)]
    load_u = pltpu.make_async_copy(u_in, ubuf.at[:, xh], loc.at[6])
    loads_sp[0].start()
    loads_st[0].start()
    load_u.start()
    loads_sp[1].start()
    loads_sp[2].start()
    loads_st[1].start()
    loads_st[2].start()

    nxt_r = lax.rem(me_r + 1, 4)
    prv_r = lax.rem(me_r + 3, 4)
    plane_peers = [(dy, dz) for dy in range(4) for dz in range(4) if (dy, dz) != (0, 0)]
    xc_peers = [(dx, dc) for dx in range(4) for dc in range(2) if (dx, dc) != (0, 0)]

    def plane_dev(dy, dz):
        return {Y: lax.rem(y + dy, 4), Z: lax.rem(z + dz, 4)}

    def xc_dev(dx, dc):
        v = lax.rem(x + dx, 4)
        return {XH: v // 2, XL: lax.rem(v, 2), CO: lax.rem(c + dc, 2)}

    barrier = pltpu.get_barrier_semaphore()
    for p in plane_peers:
        pl.semaphore_signal(barrier, inc=1, device_id=plane_dev(*p), device_id_type=MESH_ID)
    for p in xc_peers:
        pl.semaphore_signal(barrier, inc=1, device_id=xc_dev(*p), device_id_type=MESH_ID)

    nxt_dev = {XL: nxt_r // 2, CO: lax.rem(nxt_r, 2)}

    def spare_copy(i, l):
        if i == 0:
            return remote(spb.at[0, l], spr.at[0, l], sp_s.at[l], sp_r.at[l], nxt_dev)
        return remote(spb.at[i], spr.at[i], sp_s.at[1 + i], sp_r.at[1 + i], nxt_dev)

    scale_copy = remote(scs, scr, sp_s.at[4], sp_r.at[4], nxt_dev)

    def sc_copy(di, d):
        return remote(scr, scn.at[xh], sc_s.at[di], sc_r.at[di], to_x(xn[d]))

    def x_copy(k, l, di, d):
        src = x_in.at[l, :, pl.ds(pl.multiple_of(xn_h[d] * half + k * ck, ck), ck)]
        return remote(src, xbuf.at[k, l, xh], x_s.at[k, l, di], x_r.at[k, l, di], to_x(xn[d]))

    def w_copy(l, di, d):
        return remote(
            wsb.at[xn_h[d], :, l], wbuf.at[:, l, y, xh, z], w_s.at[l, di], w_r.at[l, di], to_x(xn[d])
        )

    u_far = lax.rem(x + 1 + 2 * (1 - lax.rem(x, 2)), 4)

    def u_copy(part):
        span = slice(part * (tok // 2), (part + 1) * (tok // 2))
        return remote(u_in.at[c, span], ubuf.at[c, xh, span], u_s.at[part], u_r.at[part], to_x(u_far))

    u_fwd = remote(ubuf.at[c, 1 - xh], ubuf.at[c, 1 - xh], u_s.at[2], u_r.at[2], {CO: 1 - c})

    def region(k, l, stage, p, h):
        hs = slice(None) if h is None else h
        if l == 0:
            return wbuf.at[k, 0, p, hs, z] if stage == 0 else wbuf.at[k, 0, :, hs, p]
        return wbuf.at[k, 1, y, hs, p] if stage == 0 else wbuf.at[k, 1, p, hs, :]

    def ag_copy(k, l, stage, step, di, d):
        axis = plane_axis[l][stage]
        pos = plane_pos[axis]
        ref = region(k, l, stage, pos, None) if step == 0 else region(k, l, stage, ring(pos, -d), di)
        n = stage * 2 + step
        return remote(ref, ref, ag_s.at[k, l, n, di], ag_r.at[k, l, n, di], {axis: ring(pos, d)})

    def dw_piece(k, l, p, h):
        return dwbuf.at[k, 0, :, h, p] if l == 0 else dwbuf.at[k, 1, p, h, :]

    def rs_parts(k, l, stage):
        axis = plane_axis[l][1 - stage]
        if stage == 0:
            return axis, (lambda p, h: dw_piece(k, l, p, h)), r1a, r1b, r1c
        return axis, (lambda p, h: s1.at[k, l, h, p]), r2a, r2b, r2c

    def rs_copy(k, l, stage, what, di, d):
        axis, piece, ra, rb, rc = rs_parts(k, l, stage)
        pos = plane_pos[axis]
        if what == 0:
            src, dst = piece(ring(pos, 2), di), ra.at[k, l, di]
        elif what == 1:
            src, dst = piece(ring(pos, d), 1 - di), rb.at[k, l, di]
        else:
            src, dst = ra.at[k, l, di], rc.at[k, l, di]
        n = stage * 3 + what
        return remote(src, dst, rs_s.at[k, l, n, di], rs_r.at[k, l, n, di], {axis: ring(pos, d)})

    def rs_start(k, l, stage):
        for what in (0, 1):
            for di, d in DIRS:
                rs_copy(k, l, stage, what, di, d).start()

    def each(stage, fn):
        if stage == 0:

            @pl.loop(0, 4)
            def _(j):
                fn(j)
        else:
            fn(None)

    def at(ref, j):
        return ref[j] if j is not None else ref[...]

    def rs_forward(k, l, stage):
        axis, piece, ra, rb, rc = rs_parts(k, l, stage)
        pos = plane_pos[axis]
        for di, d in DIRS:
            rs_copy(k, l, stage, 0, di, d).wait_recv()
            own = piece(ring(pos, d), di)
            acc = ra.at[k, l, di]

            def add(j, own=own, acc=acc):
                total = (at(acc, j).astype(F32) + at(own, j).astype(F32)).astype(BF)
                if j is None:
                    acc[...] = total
                else:
                    acc[j] = total

            each(stage, add)
            rs_copy(k, l, stage, 2, di, d).start()

    def rs_finish(k, l, stage):
        axis, piece, ra, rb, rc = rs_parts(k, l, stage)
        pos = plane_pos[axis]
        for what in (1, 2):
            for di, d in DIRS:
                rs_copy(k, l, stage, what, di, d).wait_recv()
        for h in range(2):
            own = piece(pos, h)
            through = rc.at[k, l, h]
            direct = rb.at[k, l, 1 - h]
            out = s1.at[k, l, h] if stage == 0 else s2.at[k, l, h]

            def add(j, own=own, through=through, direct=direct, out=out):
                total = at(own, j).astype(F32) + at(through, j).astype(F32) + at(direct, j).astype(F32)
                if j is None:
                    out[...] = total.astype(BF)
                else:
                    out[j] = total.astype(BF)

            each(stage, add)

    def g_copy(k, l, di, d):
        return remote(
            s2.at[k, l, xn_h[d]], gbuf.at[k, l, xh], g_s.at[k, l, di], g_r.at[k, l, di], to_x(xn[d])
        )

    def ig_copy(k, l, di, d):
        dst = ig_out.at[l, :, pl.ds(pl.multiple_of(xh * half + k * ck, ck), ck)]
        return remote(igb.at[k, l, xn_h[d]], dst, ig_s.at[k, l, di], ig_r.at[k, l, di], to_x(xn[d]))

    kv_core = remote(kvs, kvr, kv_s.at[0], kv_r.at[0], {CO: 1 - c})

    def kv_piece(v, l):
        return kvr.at[lax.rem(v, 2), l, v // 2]

    def kv_copy(what, di, d):
        if what == 0:
            src, dst = kv_piece(ring(x, 2), di), ka.at[di]
        elif what == 1:
            src, dst = kv_piece(ring(x, d), 1 - di), kb.at[di]
        else:
            src, dst = ka.at[di], kc.at[di]
        n = 1 + what * 2 + di
        return remote(src, dst, kv_s.at[n], kv_r.at[n], to_x(xn[d]))

    kv_store = pltpu.make_async_copy(kvo, kv_out, loc.at[7])
    np_copies = [
        remote(nsend, npl.at[i], np_s.at[i], np_r.at[i], plane_dev(*p)) for i, p in enumerate(plane_peers)
    ]
    nx_copies = [
        remote(nsend2, nxc.at[i], nx_s.at[i], nx_r.at[i], xc_dev(*p)) for i, p in enumerate(xc_peers)
    ]
    stores = [
        pltpu.make_async_copy(st.at[i], out, loc.at[8 + i]) for i, out in enumerate((nm_out, nf_out, ns_out))
    ]

    lost = jnp.broadcast_to(failed[...], (rows, ck)) == me_r

    def begin():
        loads_sp[0].wait()
        for l in range(layers):
            spb[0, l] = spf[0, l].astype(BF)
        scs[...] = jnp.broadcast_to(scale_spare[...], scs.shape)
        pl.semaphore_wait(barrier, len(plane_peers) + len(xc_peers))
        u_copy(0).start()
        for l in range(layers):
            spare_copy(0, l).start()
        scale_copy.start()
        loads_st[0].wait()

    def recover(l):
        spare_copy(0, l).wait_recv()
        for j in range(2 * NK):
            span = slice(j * ck, (j + 1) * ck)
            now = jnp.where(lost, spr[0, l, :, span].astype(F32), st[0, l, :, span])
            st[0, l, :, span] = now
            wsb[j // NK, j % NK, l] = now.astype(BF)
        for di, d in DIRS:
            w_copy(l, di, d).start()

    def exchange():
        u_copy(1).start()
        n = 0
        for k in range(NK):
            for l in range(layers):
                for di, d in DIRS:
                    x_copy(k, l, di, d).start()
                if n == SPARES_AT:
                    for i in (1, 2):
                        loads_sp[i].wait()
                        for ll in range(layers):
                            spb[i, ll] = spf[i, ll].astype(BF)
                        spare_copy(i, 0).start()
                n += 1
        scale_copy.wait_recv()
        lost_tile = jnp.broadcast_to(failed[...], scr.shape) == me_r
        scr[...] = jnp.where(lost_tile, scr[...], jnp.broadcast_to(scale_own[...], scr.shape))
        nacc[...] = jnp.zeros(nacc.shape, F32)
        load_u.wait()
        for di, d in DIRS:
            sc_copy(di, d).start()

    def forward_u():
        for part in range(2):
            u_copy(part).wait_recv()
        u_fwd.start()

    def transpose_u():
        u_fwd.wait_recv()
        for l in range(layers):

            @pl.loop(0, 4)
            def _(j):
                span = pl.ds(pl.multiple_of(j * (feats // 4), feats // 4), feats // 4)
                for t in range(2):
                    ut[l, j, :, t * tok : (t + 1) * tok] = ubuf[l, t, :, span].T

    got_w = set()

    def gather_0(k, l):
        if l not in got_w:
            got_w.add(l)
            for di, d in DIRS:
                w_copy(l, di, d).wait_recv()
        for di, d in DIRS:
            ag_copy(k, l, 0, 0, di, d).start()

    def gather_forward(stage, k, l):
        for di, d in DIRS:
            ag_copy(k, l, stage, 0, di, d).wait_recv()
            ag_copy(k, l, stage, 1, di, d).start()

    def gather_1(k, l):
        for di, d in DIRS:
            ag_copy(k, l, 0, 1, di, d).wait_recv()
        for di, d in DIRS:
            ag_copy(k, l, 1, 0, di, d).start()

    def gathered(k, l):
        for di, d in DIRS:
            ag_copy(k, l, 1, 1, di, d).wait_recv()

    got_x = set()

    def need_x(k, l):
        if (k, l) not in got_x:
            got_x.add((k, l))
            for di, d in DIRS:
                x_copy(k, l, di, d).wait_recv()

    def grad_product(k, l):
        need_x(k, l)

        @pl.loop(0, 4)
        def _(j):
            inputs = xbuf[k, l].reshape(2 * tok, ck)
            part = jnp.dot(ut[l, j], inputs, preferred_element_type=F32)
            dwbuf[k, l, j] = part.astype(BF).reshape(2, 4, rows, ck)

        rs_start(k, l, 0)

    def finish_0(k, l):
        rs_finish(k, l, 0)
        rs_start(k, l, 1)

    got_scale = set()

    def finish_1(k, l):
        rs_finish(k, l, 1)
        for di, d in DIRS:
            g_copy(k, l, di, d).start()
        if not got_scale:
            got_scale.add(1)
            for di, d in DIRS:
                sc_copy(di, d).wait_recv()
        total = jnp.zeros((rows, ck), F32)
        for h in range(2):
            grad = s2[k, l, h].astype(F32) / jnp.broadcast_to(scn[h, 0:1, 0:1], (rows, ck))
            total = total + grad * grad
        nacc[...] += total

    kv_begun = set()

    def kv_product(k, l):
        need_x(k, l)
        fresh = l not in kv_begun
        kv_begun.add(l)

        @pl.loop(0, 4)
        def _(j):
            inputs = xbuf[k, l].reshape(2 * tok, ck)
            weight = wbuf[k, l, j].reshape(8 * rows, ck)
            part = lax.dot_general(
                inputs, weight, (((1,), (1,)), ((), ())), preferred_element_type=F32
            ).reshape(2, tok, 8 * rows)
            if fresh:
                kvp[j, l] = part
            else:
                kvp[j, l] += part

    def ig_product(k, l):
        @pl.loop(0, 2)
        def _(t):
            weight = wbuf[k, l].reshape(feats, ck)
            igb[k, l, t] = jnp.dot(ubuf[l, t], weight, preferred_element_type=F32).astype(BF)

        for di, d in DIRS:
            ig_copy(k, l, di, d).start()

    def kv_cores():
        for v in range(2):
            kvs[v] = kvp[2 * v + (1 - c)].astype(BF)
        kv_core.start()

    def kv_ring():
        kv_core.wait_recv()
        for v in range(2):
            for l in range(layers):
                kvr[v, l] = (kvr[v, l].astype(F32) + kvp[2 * v + c, l]).astype(BF)
        for what in (0, 1):
            for di, d in DIRS:
                kv_copy(what, di, d).start()

    def kv_forward():
        for di, d in DIRS:
            kv_copy(0, di, d).wait_recv()
            ka[di] = (ka[di].astype(F32) + kv_piece(ring(x, d), di)[...].astype(F32)).astype(BF)
            kv_copy(2, di, d).start()

    def kv_finish():
        for what in (1, 2):
            for di, d in DIRS:
                kv_copy(what, di, d).wait_recv()
        for h in range(2):
            own = kv_piece(x, h)[...].astype(F32)
            kvo[h] = (own + kc[h].astype(F32) + kb[1 - h].astype(F32)).astype(BF)
        kv_store.start()

    def squares_plane():
        tile = jnp.zeros((8, 128), F32)
        for i in range(rows // 8):
            for j in range(ck // 128):
                tile = tile + nacc[8 * i : 8 * i + 8, 128 * j : 128 * j + 128]
        nsend[...] = tile
        for cp in np_copies:
            cp.start()

    def squares_rest():
        total = nsend[...]
        for i, cp in enumerate(np_copies):
            cp.wait_recv()
            total = total + npl[i]
        nsend2[...] = total
        for cp in nx_copies:
            cp.start()

    def adam():
        for i in (1, 2):
            loads_st[i].wait()
            spare_copy(i, 0).wait_recv()
        for k in range(NK):
            for l in range(layers):
                for di, d in DIRS:
                    g_copy(k, l, di, d).wait_recv()
        total = nsend2[...]
        for i, cp in enumerate(nx_copies):
            cp.wait_recv()
            total = total + nxc[i]
        squares = jnp.sum(jnp.sum(total, axis=1, keepdims=True), axis=0, keepdims=True)
        factor = jnp.minimum(1.0, lax.rsqrt(squares / entries + MEAN_EPS))
        factor = jnp.broadcast_to(factor, (rows, ck))
        scale = jnp.broadcast_to(scr[0:1, 0:1], (rows, ck))

        @pl.loop(0, 2 * NK)
        def _(j):
            span = pl.ds(pl.multiple_of(j * ck, ck), ck)
            h = j // NK
            k = lax.rem(j, NK)
            for l in range(layers):
                clipped = gbuf[k, l, h].astype(F32) / scale * factor
                first_now = jnp.where(lost, spr[1, l, :, span].astype(F32), st[1, l, :, span])
                second_now = jnp.where(lost, spr[2, l, :, span].astype(F32), st[2, l, :, span])
                master_now = st[0, l, :, span]
                new_first = BETA_FIRST * first_now + (1.0 - BETA_FIRST) * clipped
                new_second = BETA_SECOND * second_now + (1.0 - BETA_SECOND) * clipped * clipped
                st[0, l, :, span] = master_now - LEARN_RATE * (
                    new_first / (jnp.sqrt(new_second) + ADAM_EPS) + DECAY_RATE * master_now
                )
                st[1, l, :, span] = new_first
                st[2, l, :, span] = new_second

        for cp in stores:
            cp.start()

    steps = {
        "INI": begin,
        "WSEL": recover,
        "XREST": exchange,
        "UF": forward_u,
        "TR": transpose_u,
        "A1": gather_0,
        "F0": functools.partial(gather_forward, 0),
        "S1": gather_1,
        "F1": functools.partial(gather_forward, 1),
        "WD": gathered,
        "DW": grad_product,
        "RF0": lambda k, l: rs_forward(k, l, 0),
        "RE0": finish_0,
        "RF1": lambda k, l: rs_forward(k, l, 1),
        "RE1": finish_1,
        "KV": kv_product,
        "IG": ig_product,
        "KVC": kv_cores,
        "KVA": kv_ring,
        "KVF": kv_forward,
        "KVE": kv_finish,
        "SQ": squares_plane,
        "NX": squares_rest,
        "AD": adam,
        "END": lambda: None,
    }
    for name, *where in ORDER:
        steps[name](*where)

    for l in range(layers):
        spare_copy(0, l).wait_send()
    for i in (1, 2):
        spare_copy(i, 0).wait_send()
    scale_copy.wait_send()
    for part in range(2):
        u_copy(part).wait_send()
    for di, d in DIRS:
        sc_copy(di, d).wait_send()
    u_fwd.wait_send()
    kv_core.wait_send()
    for l in range(layers):
        for di, d in DIRS:
            w_copy(l, di, d).wait_send()
    for what in range(3):
        for di, d in DIRS:
            kv_copy(what, di, d).wait_send()
    for cp in np_copies + nx_copies:
        cp.wait_send()

    @pl.loop(0, NK)
    def _(k):
        for l in range(layers):
            for di, d in DIRS:
                x_copy(k, l, di, d).wait_send()
                ig_copy(k, l, di, d).wait_send()
                g_copy(k, l, di, d).wait_send()
                for stage in range(2):
                    for step in range(2):
                        ag_copy(k, l, stage, step, di, d).wait_send()
                    for what in range(3):
                        rs_copy(k, l, stage, what, di, d).wait_send()
                ig_copy(k, l, di, d).wait_recv()

    kv_store.wait()
    for cp in stores:
        cp.wait()


def local(
    layer_input,
    kv_cotangent,
    failed_member,
    master,
    first_moment,
    second_moment,
    loss_scale,
    spare_master,
    spare_first,
    spare_second,
    spare_scale,
):
    layers, tok, cols = layer_input.shape
    rows = master.shape[1]
    feats = kv_cotangent.shape[2]
    half = cols // 2
    ck = half // NK
    entries = float(layers * rows * lax.axis_size(FSDP) * cols * lax.axis_size(RED))
    any_ = pl.BlockSpec(memory_space=pl.ANY)
    vmem = pl.BlockSpec(memory_space=pltpu.VMEM)
    sem = pltpu.SemaphoreType.DMA
    scratch = [
        pltpu.VMEM((NK, layers, 2, tok, ck), BF),
        pltpu.VMEM((layers, 2, tok, feats), BF),
        pltpu.VMEM((layers, 4, feats // 4, 2 * tok), BF),
        pltpu.VMEM((2, NK, layers, rows, ck), BF),
        pltpu.VMEM((NK, layers, 4, 2, 4, rows, ck), BF),
        pltpu.VMEM((NK, layers, 4, 2, 4, rows, ck), BF),
        pltpu.VMEM((NK, layers, 2, 4, rows, ck), BF),
        pltpu.VMEM((NK, layers, 2, 4, rows, ck), BF),
        pltpu.VMEM((NK, layers, 2, 4, rows, ck), BF),
        pltpu.VMEM((NK, layers, 2, 4, rows, ck), BF),
        pltpu.VMEM((NK, layers, 2, rows, ck), BF),
        pltpu.VMEM((NK, layers, 2, rows, ck), BF),
        pltpu.VMEM((NK, layers, 2, rows, ck), BF),
        pltpu.VMEM((NK, layers, 2, rows, ck), BF),
        pltpu.VMEM((NK, layers, 2, rows, ck), BF),
        pltpu.VMEM((NK, layers, 2, tok, ck), BF),
        pltpu.VMEM((4, layers, 2, tok, feats // 4), F32),
        pltpu.VMEM((2, layers, 2, tok, feats // 4), BF),
        pltpu.VMEM((2, layers, 2, tok, feats // 4), BF),
        pltpu.VMEM((2, tok, feats // 4), BF),
        pltpu.VMEM((2, tok, feats // 4), BF),
        pltpu.VMEM((2, tok, feats // 4), BF),
        pltpu.VMEM((2, tok, feats // 4), BF),
        pltpu.VMEM((3, layers, rows, cols), F32),
        pltpu.VMEM((3, layers, rows, cols), F32),
        pltpu.VMEM((3, layers, rows, cols), BF),
        pltpu.VMEM((3, layers, rows, cols), BF),
        pltpu.VMEM((8, 128), F32),
        pltpu.VMEM((8, 128), F32),
        pltpu.VMEM((2, 8, 128), F32),
        pltpu.VMEM((rows, ck), F32),
        pltpu.VMEM((8, 128), F32),
        pltpu.VMEM((15, 8, 128), F32),
        pltpu.VMEM((8, 128), F32),
        pltpu.VMEM((7, 8, 128), F32),
        sem((11,)),
        sem((5,)),
        sem((5,)),
        sem((3,)),
        sem((3,)),
        sem((NK, layers, 2)),
        sem((NK, layers, 2)),
        sem((layers, 2)),
        sem((layers, 2)),
        sem((NK, layers, 4, 2)),
        sem((NK, layers, 4, 2)),
        sem((NK, layers, 6, 2)),
        sem((NK, layers, 6, 2)),
        sem((NK, layers, 2)),
        sem((NK, layers, 2)),
        sem((NK, layers, 2)),
        sem((NK, layers, 2)),
        sem((7,)),
        sem((7,)),
        sem((15,)),
        sem((15,)),
        sem((7,)),
        sem((7,)),
        sem((2,)),
        sem((2,)),
    ]
    return pl.pallas_call(
        functools.partial(kernel, entries),
        out_shape=(
            jax.ShapeDtypeStruct((layers, tok, feats // 4), BF),
            jax.ShapeDtypeStruct((layers, tok, cols), BF),
            jax.ShapeDtypeStruct(master.shape, F32),
            jax.ShapeDtypeStruct(master.shape, F32),
            jax.ShapeDtypeStruct(master.shape, F32),
        ),
        in_specs=[any_, any_, vmem, vmem, vmem] + [any_] * 6,
        out_specs=(any_,) * 5,
        scratch_shapes=scratch,
        compiler_params=pltpu.CompilerParams(
            collective_id=0, has_side_effects=True, vmem_limit_bytes=67043328
        ),
        name="restore_step",
    )(
        layer_input,
        kv_cotangent,
        failed_member.reshape(1, 1),
        loss_scale,
        spare_scale,
        master,
        first_moment,
        second_moment,
        spare_master,
        spare_first,
        spare_second,
    )


def solution(mesh):
    split = Mesh(mesh.devices.reshape(4, 2, 4, 2, 2), (Y, XH, Z, XL, CO))
    placed = (
        P(None, FSDP, RED),
        P(None, FSDP, None),
        P(FSDP),
        P(None, FSDP, RED),
        P(None, FSDP, RED),
        P(None, FSDP, RED),
        P(FSDP, RED),
        P(None, FSDP, RED),
        P(None, FSDP, RED),
        P(None, FSDP, RED),
        P(FSDP, RED),
    )
    return jax.shard_map(
        local,
        mesh=split,
        in_specs=placed,
        out_specs=(P(None, FSDP, RED),) * 5,
        check_vma=False,
    )
```

time: 177 us -> 154 us (0.87)
  Pallas kernels: 165 us -> 142 us
    pallas_call x1, Pallas kernels: 165 us -> 142 us  [local(): pl.pallas_call(functools.partial(kernel, entries), out_shape=(jax.ShapeDt...]
where the time goes in v2:
time: 154 us
  Pallas kernels  142 us (92%)
  local copies, waits for them, and re-layouts  9.44 us (6%)
  between operations  2.59 us (2%)
    pallas_call x1, Pallas kernels, local(): pl.pallas_call(functools.partial(kernel, entries), out_shape=(jax.ShapeDt...  142 us
    unnamed x11, local copies, waits for them, and re-layouts  9.44 us

profile of v2, /device:TPU:1, one launch (start us, length us, event | category | flops | bytes accessed | tf_op | source)
XLA Modules:
  0.0 153.9 jit_solution(12180402192165916458)
XLA Ops:
  2.6 141.8 %restore_step.1 = (bf16[2,256,256]{2,1,0:T(8,128)(2,1)}, bf16[2,256,4096]{2,1,0:T(8,128)(2,1)}, f32[2,32,4096]{2,1,0:T(8,128)}, f32[2,32,4096]{2,1,0:T(8,128)}, f32[2,32,4096]{2,1,0:T(8,128)}) custom-call(bf16[2,256,4096]{2,1,0:T(8,128)(2,1)} %x_in.1, bf16[2,256,1024]{2,1,0:T(8,128)(2,1)} %u_in.1, s32[1,1]{1,0:T(1,128)} %bitcast.1.failed, ...), custom_call_target="tpu_custom_call" | custom-call | tf_op jit(solution)/shard_map/restore_step/pallas_call | solution.py:825
  144.4 1.7 %copy.24 = bf16[2,256,256]{2,1,0:T(8,128)(2,1)} copy(bf16[2,256,256]{2,1,0:T(8,128)(2,1)} %get-tuple-element.10) | data formatting | bytes 524288
  146.1 0.0 copy-start.2
  146.1 0.0 copy-start.1
  146.1 4.8 %copy.25 = bf16[2,256,4096]{2,1,0:T(8,128)(2,1)} copy(bf16[2,256,4096]{2,1,0:T(8,128)(2,1)} %get-tuple-element.11) | data formatting | bytes 8388608
  150.9 0.0 copy-done.2
  150.9 0.0 copy-start
  150.9 1.0 copy.26
  151.9 0.0 copy-done.1
  151.9 1.0 copy.27
  152.9 0.0 copy-done
  152.9 1.0 copy.28
Async XLA Ops:
  146.1 4.9 %copy-start.2 = (f32[2,32,4096]{2,1,0:T(8,128)S(1)}, f32[2,32,4096]{2,1,0:T(8,128)}, u32[]{:S(2)}) copy-start(f32[2,32,4096]{2,1,0:T(8,128)} %get-tuple-element.12) | copy-start | bytes 3145732
  146.1 5.8 %copy-start.1 = (f32[2,32,4096]{2,1,0:T(8,128)S(1)}, f32[2,32,4096]{2,1,0:T(8,128)}, u32[]{:S(2)}) copy-start(f32[2,32,4096]{2,1,0:T(8,128)} %get-tuple-element.13) | copy-start | bytes 3145732
  150.9 1.9 %copy-start = (f32[2,32,4096]{2,1,0:T(8,128)S(1)}, f32[2,32,4096]{2,1,0:T(8,128)}, u32[]{:S(2)}) copy-start(f32[2,32,4096]{2,1,0:T(8,128)} %get-tuple-element.14) | copy-start | bytes 3145732

commit v3 on v2

--- a/solution.py
+++ b/solution.py
@@ -178,8 +178,6 @@
     ka,
     kb,
     kc,
-    kvo,
-    st,
     spf,
     spb,
     spr,
@@ -247,9 +245,10 @@
         )
 
     states = (master, first, second)
+    st = (nm_out, nf_out, ns_out)
     spares = (sp_master, sp_first, sp_second)
     loads_sp = [pltpu.make_async_copy(spares[i], spf.at[i], loc.at[i]) for i in range(3)]
-    loads_st = [pltpu.make_async_copy(states[i], st.at[i], loc.at[3 + i]) for i in range(3)]
+    loads_st = [pltpu.make_async_copy(states[i], st[i], loc.at[3 + i]) for i in range(3)]
     load_u = pltpu.make_async_copy(u_in, ubuf.at[:, xh], loc.at[6])
     loads_sp[0].start()
     loads_st[0].start()
@@ -420,15 +419,11 @@
         n = 1 + what * 2 + di
         return remote(src, dst, kv_s.at[n], kv_r.at[n], to_x(xn[d]))
 
-    kv_store = pltpu.make_async_copy(kvo, kv_out, loc.at[7])
     np_copies = [
         remote(nsend, npl.at[i], np_s.at[i], np_r.at[i], plane_dev(*p)) for i, p in enumerate(plane_peers)
     ]
     nx_copies = [
         remote(nsend2, nxc.at[i], nx_s.at[i], nx_r.at[i], xc_dev(*p)) for i, p in enumerate(xc_peers)
-    ]
-    stores = [
-        pltpu.make_async_copy(st.at[i], out, loc.at[8 + i]) for i, out in enumerate((nm_out, nf_out, ns_out))
     ]
 
     lost = jnp.broadcast_to(failed[...], (rows, ck)) == me_r
@@ -449,8 +444,8 @@
         spare_copy(0, l).wait_recv()
         for j in range(2 * NK):
             span = slice(j * ck, (j + 1) * ck)
-            now = jnp.where(lost, spr[0, l, :, span].astype(F32), st[0, l, :, span])
-            st[0, l, :, span] = now
+            now = jnp.where(lost, spr[0, l, :, span].astype(F32), st[0][l, :, span])
+            st[0][l, :, span] = now
             wsb[j // NK, j % NK, l] = now.astype(BF)
         for di, d in DIRS:
             w_copy(l, di, d).start()
@@ -610,8 +605,7 @@
                 kv_copy(what, di, d).wait_recv()
         for h in range(2):
             own = kv_piece(x, h)[...].astype(F32)
-            kvo[h] = (own + kc[h].astype(F32) + kb[1 - h].astype(F32)).astype(BF)
-        kv_store.start()
+            kv_out[h] = (own + kc[h].astype(F32) + kb[1 - h].astype(F32)).astype(BF)
 
     def squares_plane():
         tile = jnp.zeros((8, 128), F32)
@@ -655,19 +649,16 @@
             k = lax.rem(j, NK)
             for l in range(layers):
                 clipped = gbuf[k, l, h].astype(F32) / scale * factor
-                first_now = jnp.where(lost, spr[1, l, :, span].astype(F32), st[1, l, :, span])
-                second_now = jnp.where(lost, spr[2, l, :, span].astype(F32), st[2, l, :, span])
-                master_now = st[0, l, :, span]
+                first_now = jnp.where(lost, spr[1, l, :, span].astype(F32), st[1][l, :, span])
+                second_now = jnp.where(lost, spr[2, l, :, span].astype(F32), st[2][l, :, span])
+                master_now = st[0][l, :, span]
                 new_first = BETA_FIRST * first_now + (1.0 - BETA_FIRST) * clipped
                 new_second = BETA_SECOND * second_now + (1.0 - BETA_SECOND) * clipped * clipped
-                st[0, l, :, span] = master_now - LEARN_RATE * (
+                st[0][l, :, span] = master_now - LEARN_RATE * (
                     new_first / (jnp.sqrt(new_second) + ADAM_EPS) + DECAY_RATE * master_now
                 )
-                st[1, l, :, span] = new_first
-                st[2, l, :, span] = new_second
-
-        for cp in stores:
-            cp.start()
+                st[1][l, :, span] = new_first
+                st[2][l, :, span] = new_second
 
     steps = {
         "INI": begin,
@@ -733,8 +724,13 @@
                         rs_copy(k, l, stage, what, di, d).wait_send()
                 ig_copy(k, l, di, d).wait_recv()
 
-    kv_store.wait()
-    for cp in stores:
+
+def store(*refs):
+    sems = refs[10]
+    copies = [pltpu.make_async_copy(refs[i], refs[5 + i], sems.at[i]) for i in range(5)]
+    for cp in copies:
+        cp.start()
+    for cp in copies:
         cp.wait()
 
 
@@ -783,8 +779,6 @@
         pltpu.VMEM((2, tok, feats // 4), BF),
         pltpu.VMEM((2, tok, feats // 4), BF),
         pltpu.VMEM((2, tok, feats // 4), BF),
-        pltpu.VMEM((2, tok, feats // 4), BF),
-        pltpu.VMEM((3, layers, rows, cols), F32),
         pltpu.VMEM((3, layers, rows, cols), F32),
         pltpu.VMEM((3, layers, rows, cols), BF),
         pltpu.VMEM((3, layers, rows, cols), BF),
@@ -796,7 +790,7 @@
         pltpu.VMEM((15, 8, 128), F32),
         pltpu.VMEM((8, 128), F32),
         pltpu.VMEM((7, 8, 128), F32),
-        sem((11,)),
+        sem((7,)),
         sem((5,)),
         sem((5,)),
         sem((3,)),
@@ -822,20 +816,18 @@
         sem((2,)),
         sem((2,)),
     ]
-    return pl.pallas_call(
+    results = (
+        jax.ShapeDtypeStruct((layers, tok, feats // 4), BF),
+        jax.ShapeDtypeStruct((layers, tok, cols), BF),
+    ) + (jax.ShapeDtypeStruct(master.shape, F32),) * 3
+    held = pl.pallas_call(
         functools.partial(kernel, entries),
-        out_shape=(
-            jax.ShapeDtypeStruct((layers, tok, feats // 4), BF),
-            jax.ShapeDtypeStruct((layers, tok, cols), BF),
-            jax.ShapeDtypeStruct(master.shape, F32),
-            jax.ShapeDtypeStruct(master.shape, F32),
-            jax.ShapeDtypeStruct(master.shape, F32),
-        ),
+        out_shape=tuple(pltpu.VMEM(r.shape, r.dtype) for r in results),
         in_specs=[any_, any_, vmem, vmem, vmem] + [any_] * 6,
-        out_specs=(any_,) * 5,
+        out_specs=(vmem,) * 5,
         scratch_shapes=scratch,
         compiler_params=pltpu.CompilerParams(
-            collective_id=0, has_side_effects=True, vmem_limit_bytes=67043328
+            collective_id=0, has_side_effects=True, vmem_limit_bytes=55 << 20
         ),
         name="restore_step",
     )(
@@ -851,6 +843,15 @@
         spare_first,
         spare_second,
     )
+    return pl.pallas_call(
+        store,
+        out_shape=results,
+        in_specs=[vmem] * 5,
+        out_specs=(any_,) * 5,
+        scratch_shapes=[sem((5,))],
+        compiler_params=pltpu.CompilerParams(vmem_limit_bytes=1 << 20),
+        name="store_results",
+    )(*[pltpu.with_memory_space_constraint(h, pltpu.VMEM) for h in held])
 
 
 def solution(mesh):

time: 154 us -> 147 us (0.955)
  local copies, waits for them, and re-layouts: 9.44 us -> 0 us
  Pallas kernels: 142 us -> 145 us
    unnamed x11 -> x0, local copies, waits for them, and re-layouts: 9.44 us -> none
    pallas_call x1 -> x2, Pallas kernels: 142 us -> 145 us  [the longest x1 142 us: local(): pl.pallas_call(functools.partial(kernel, entries), out_shape=tuple((pltpu...]
where the time goes in v3:
time: 147 us
  Pallas kernels  145 us (99%)
  between operations  2.58 us (2%)
    pallas_call x1, Pallas kernels, local(): pl.pallas_call(functools.partial(kernel, entries), out_shape=tuple((pltpu...  142 us
    pallas_call x1, Pallas kernels, local(): pl.pallas_call(store, out_shape=results, in_specs=[vmem] * 5, out_specs=(...  3.11 us

profile of v3, /device:TPU:1, one launch (start us, length us, event | category | flops | bytes accessed | tf_op | source)
XLA Modules:
  0.0 147.2 jit_solution(9543593449275094644)
XLA Ops:
  2.6 141.5 %restore_step.1 = (bf16[2,256,256]{2,1,0:T(8,128)(2,1)S(1)}, bf16[2,256,4096]{2,1,0:T(8,128)(2,1)S(1)}, f32[2,32,4096]{2,1,0:T(8,128)S(1)}, f32[2,32,4096]{2,1,0:T(8,128)S(1)}, f32[2,32,4096]{2,1,0:T(8,128)S(1)}) custom-call(bf16[2,256,4096]{2,1,0:T(8,128)(2,1)} %x_in.1, bf16[2,256,1024]{2,1,0:T(8,128)(2,1)} %u_in.1, s32[1,1]{1,0:T(1,128)} %bitcast.1.failed, ...), custom_call_target="tpu_custom_call" | custom-call | tf_op jit(solution)/shard_map/restore_step/pallas_call | solution.py:823
  144.1 3.1 %store_results.1 = (bf16[2,256,256]{2,1,0:T(8,128)(2,1)}, bf16[2,256,4096]{2,1,0:T(8,128)(2,1)}, f32[2,32,4096]{2,1,0:T(8,128)}, f32[2,32,4096]{2,1,0:T(8,128)}, f32[2,32,4096]{2,1,0:T(8,128)}) custom-call(bf16[2,256,256]{2,1,0:T(8,128)(2,1)S(1)} %get-tuple-element.10.refs_0_, bf16[2,256,4096]{2,1,0:T(8,128)(2,1)S(1)} %get-tuple-element.11.refs_1_, ...), custom_call_target="tpu_custom_call" | custom-call | tf_op jit(solution)/shard_map/store_results/pallas_call | solution.py:846

commit v4 on v3

--- a/solution.py
+++ b/solution.py
@@ -21,7 +21,10 @@
 MEAN_EPS = 1e-06
 
 NK = 4
-SPARES_AT = 4
+WID = (512, 512, 512, 256)
+OFF = tuple(sum(WID[:k]) for k in range(NK))
+EW = 512
+SPARES_AT = 0
 ORDER = (
     ("INI",),
     ("WSEL", 0),
@@ -31,108 +34,134 @@
     ("A1", 1, 0),
     ("A1", 2, 0),
     ("A1", 3, 0),
+    ("A1", 4, 0),
+    ("F0", 0, 0),
     ("A1", 0, 1),
     ("A1", 1, 1),
     ("A1", 2, 1),
     ("A1", 3, 1),
-    ("F0", 0, 0),
     ("F0", 1, 0),
+    ("A1", 4, 1),
     ("F0", 2, 0),
+    ("F0", 3, 0),
     ("F0", 0, 1),
-    ("F0", 3, 0),
+    ("UF",),
+    ("F0", 4, 0),
     ("F0", 1, 1),
     ("S1", 0, 0),
-    ("UF",),
     ("S1", 1, 0),
     ("F0", 2, 1),
     ("S1", 2, 0),
+    ("TR",),
+    ("F0", 4, 1),
+    ("S1", 4, 0),
+    ("F0", 3, 1),
+    ("S1", 0, 1),
+    ("DW", 4, 1),
+    ("S1", 1, 1),
+    ("DW", 4, 0),
     ("S1", 3, 0),
-    ("F0", 3, 1),
-    ("TR",),
-    ("S1", 0, 1),
-    ("S1", 1, 1),
     ("DW", 0, 0),
     ("F1", 0, 0),
-    ("DW", 0, 1),
     ("F1", 0, 1),
+    ("RF0", 4, 1),
     ("F1", 1, 0),
     ("S1", 2, 1),
+    ("DW", 0, 1),
+    ("F1", 2, 0),
+    ("F1", 1, 1),
+    ("S1", 4, 1),
     ("DW", 1, 0),
-    ("F1", 1, 1),
+    ("WD", 0, 1),
+    ("IG", 0, 1),
+    ("KV", 0, 1),
+    ("F1", 4, 0),
+    ("RE0", 4, 1),
+    ("S1", 3, 1),
+    ("DW", 1, 1),
+    ("RF0", 4, 0),
+    ("F1", 2, 1),
+    ("DW", 2, 0),
     ("RF0", 0, 1),
-    ("F1", 2, 0),
-    ("DW", 1, 1),
-    ("WD", 0, 1),
-    ("KV", 0, 1),
-    ("IG", 0, 1),
-    ("S1", 3, 1),
     ("F1", 3, 0),
-    ("DW", 2, 0),
     ("RF0", 0, 0),
-    ("F1", 2, 1),
+    ("DW", 2, 1),
     ("WD", 1, 1),
+    ("IG", 1, 1),
     ("KV", 1, 1),
-    ("IG", 1, 1),
+    ("DW", 3, 0),
     ("WD", 0, 0),
+    ("IG", 0, 0),
     ("KV", 0, 0),
-    ("RE0", 0, 1),
+    ("F1", 4, 1),
     ("WD", 1, 0),
+    ("IG", 1, 0),
+    ("DW", 3, 1),
+    ("F1", 3, 1),
+    ("WD", 2, 0),
+    ("IG", 2, 0),
     ("KV", 1, 0),
     ("RF0", 1, 1),
-    ("IG", 0, 0),
     ("RF0", 1, 0),
-    ("IG", 1, 0),
-    ("DW", 2, 1),
-    ("DW", 3, 0),
-    ("WD", 2, 0),
     ("KV", 2, 0),
-    ("IG", 2, 0),
-    ("F1", 3, 1),
-    ("WD", 3, 0),
-    ("KV", 3, 0),
-    ("IG", 3, 0),
     ("WD", 2, 1),
+    ("IG", 2, 1),
+    ("WD", 4, 0),
+    ("RF1", 4, 1),
+    ("IG", 4, 0),
+    ("RE0", 0, 1),
+    ("KV", 4, 0),
+    ("RE0", 4, 0),
+    ("RF0", 2, 1),
     ("KV", 2, 1),
     ("RF0", 2, 0),
-    ("RE0", 1, 1),
-    ("IG", 2, 1),
-    ("DW", 3, 1),
-    ("RF0", 2, 1),
+    ("WD", 4, 1),
+    ("IG", 4, 1),
+    ("WD", 3, 0),
+    ("KV", 4, 1),
+    ("RF0", 3, 1),
+    ("KV", 3, 0),
     ("RE0", 0, 0),
-    ("RF1", 0, 1),
     ("WD", 3, 1),
     ("KV", 3, 1),
     ("KVC",),
+    ("RF0", 3, 0),
+    ("RE0", 1, 1),
+    ("RF1", 4, 0),
     ("RE0", 1, 0),
-    ("RF0", 3, 1),
-    ("RF0", 3, 0),
+    ("RE1", 4, 1),
     ("KVA",),
+    ("RF1", 0, 1),
     ("RE0", 2, 1),
+    ("RE0", 3, 1),
+    ("RF1", 0, 0),
+    ("FE", 1),
     ("RE0", 2, 0),
-    ("RF1", 0, 0),
+    ("RE1", 4, 0),
+    ("RE0", 3, 0),
+    ("RF1", 1, 0),
+    ("KVF",),
     ("RF1", 1, 1),
-    ("RF1", 1, 0),
+    ("RE1", 0, 0),
     ("RE1", 0, 1),
-    ("RE0", 3, 0),
-    ("RE0", 3, 1),
+    ("RF1", 2, 0),
     ("RF1", 2, 1),
-    ("RF1", 2, 0),
+    ("RF1", 3, 0),
+    ("RF1", 3, 1),
+    ("RE1", 1, 0),
     ("RE1", 1, 1),
-    ("RE1", 0, 0),
-    ("RE1", 1, 0),
-    ("RF1", 3, 1),
-    ("RF1", 3, 0),
+    ("RE1", 2, 0),
+    ("FE", 0),
     ("RE1", 2, 1),
-    ("RE1", 2, 0),
+    ("RE1", 3, 0),
     ("RE1", 3, 1),
-    ("RE1", 3, 0),
     ("SQ",),
+    ("KVE",),
     ("NX",),
     ("IG", 3, 1),
-    ("KVF",),
+    ("IG", 3, 0),
     ("AD",),
     ("END",),
-    ("KVE",),
 )
 BF = jnp.bfloat16
 F32 = jnp.float32
@@ -142,9 +171,9 @@
     entries,
     x_in,
     u_in,
-    failed,
-    scale_own,
-    scale_spare,
+    failed_in,
+    scale_own_in,
+    scale_spare_in,
     master,
     first,
     second,
@@ -157,6 +186,7 @@
     nf_out,
     ns_out,
     xbuf,
+    xe,
     ubuf,
     ut,
     wsb,
@@ -171,6 +201,8 @@
     r2c,
     s2,
     gbuf,
+    grc,
+    ge,
     igb,
     kvp,
     kvs,
@@ -181,6 +213,7 @@
     spf,
     spb,
     spr,
+    small,
     scs,
     scr,
     scn,
@@ -198,6 +231,10 @@
     x_r,
     w_s,
     w_r,
+    we_s,
+    we_r,
+    ge_s,
+    ge_r,
     ag_s,
     ag_r,
     rs_s,
@@ -217,9 +254,10 @@
 ):
     layers, tok, cols = x_in.shape
     half = cols // 2
-    ck = half // NK
     rows = master.shape[1]
     feats = u_in.shape[2]
+    kept = half - EW // 2
+    failed, scale_own, scale_spare = small[0], small[1], small[2]
     y, xh, z, xl, c = (lax.axis_index(a) for a in (Y, XH, Z, XL, CO))
     x = 2 * xh + xl
     me_r = 2 * xl + c
@@ -247,14 +285,30 @@
     states = (master, first, second)
     st = (nm_out, nf_out, ns_out)
     spares = (sp_master, sp_first, sp_second)
-    loads_sp = [pltpu.make_async_copy(spares[i], spf.at[i], loc.at[i]) for i in range(3)]
+    loads_sp = [pltpu.make_async_copy(spares[i], spf, loc.at[i]) for i in range(3)]
     loads_st = [pltpu.make_async_copy(states[i], st[i], loc.at[3 + i]) for i in range(3)]
     load_u = pltpu.make_async_copy(u_in, ubuf.at[:, xh], loc.at[6])
+    load_small = [
+        pltpu.make_async_copy(ref, buf, loc.at[7 + i])
+        for i, (ref, buf) in enumerate(
+            ((failed_in, small[0]), (scale_own_in, small[1]), (scale_spare_in, small[2]))
+        )
+    ]
+    load_xe = [
+        pltpu.make_async_copy(
+            x_in.at[:, :, h * half + kept : (h + 1) * half],
+            xe.at[:, :, h * (EW // 2) : (h + 1) * (EW // 2)],
+            loc.at[10 + h],
+        )
+        for h in range(2)
+    ]
     loads_sp[0].start()
     loads_st[0].start()
+    for cp in load_small:
+        cp.start()
     load_u.start()
-    loads_sp[1].start()
-    loads_sp[2].start()
+    for cp in load_xe:
+        cp.start()
     loads_st[1].start()
     loads_st[2].start()
 
@@ -289,13 +343,21 @@
         return remote(scr, scn.at[xh], sc_s.at[di], sc_r.at[di], to_x(xn[d]))
 
     def x_copy(k, l, di, d):
-        src = x_in.at[l, :, pl.ds(pl.multiple_of(xn_h[d] * half + k * ck, ck), ck)]
-        return remote(src, xbuf.at[k, l, xh], x_s.at[k, l, di], x_r.at[k, l, di], to_x(xn[d]))
-
-    def w_copy(l, di, d):
-        return remote(
-            wsb.at[xn_h[d], :, l], wbuf.at[:, l, y, xh, z], w_s.at[l, di], w_r.at[l, di], to_x(xn[d])
-        )
+        src = x_in.at[l, :, pl.ds(pl.multiple_of(xn_h[d] * half + OFF[k], 128), WID[k])]
+        return remote(src, xbuf[k].at[l, xh], x_s.at[k, l, di], x_r.at[k, l, di], to_x(xn[d]))
+
+    def w_copy(k, l, di, d):
+        src = wsb.at[xn_h[d], l, :, OFF[k] : OFF[k] + WID[k]]
+        return remote(src, wbuf[k].at[l, y, xh, z], w_s.at[k, l, di], w_r.at[k, l, di], to_x(xn[d]))
+
+    x_far = to_x(ring(x, 2))
+
+    def we_copy(l):
+        own = wbuf[NK].at[l, y, xh, z]
+        return remote(own, own, we_s.at[l], we_r.at[l], x_far)
+
+    def ge_copy(l):
+        return remote(s2[NK].at[l, 1 - xh], grc.at[l], ge_s.at[l], ge_r.at[l], x_far)
 
     u_far = lax.rem(x + 1 + 2 * (1 - lax.rem(x, 2)), 4)
 
@@ -308,8 +370,8 @@
     def region(k, l, stage, p, h):
         hs = slice(None) if h is None else h
         if l == 0:
-            return wbuf.at[k, 0, p, hs, z] if stage == 0 else wbuf.at[k, 0, :, hs, p]
-        return wbuf.at[k, 1, y, hs, p] if stage == 0 else wbuf.at[k, 1, p, hs, :]
+            return wbuf[k].at[0, p, hs, z] if stage == 0 else wbuf[k].at[0, :, hs, p]
+        return wbuf[k].at[1, y, hs, p] if stage == 0 else wbuf[k].at[1, p, hs, :]
 
     def ag_copy(k, l, stage, step, di, d):
         axis = plane_axis[l][stage]
@@ -319,23 +381,23 @@
         return remote(ref, ref, ag_s.at[k, l, n, di], ag_r.at[k, l, n, di], {axis: ring(pos, d)})
 
     def dw_piece(k, l, p, h):
-        return dwbuf.at[k, 0, :, h, p] if l == 0 else dwbuf.at[k, 1, p, h, :]
+        return dwbuf[k].at[0, :, h, p] if l == 0 else dwbuf[k].at[1, p, h, :]
 
     def rs_parts(k, l, stage):
         axis = plane_axis[l][1 - stage]
         if stage == 0:
-            return axis, (lambda p, h: dw_piece(k, l, p, h)), r1a, r1b, r1c
-        return axis, (lambda p, h: s1.at[k, l, h, p]), r2a, r2b, r2c
+            return axis, (lambda p, h: dw_piece(k, l, p, h)), r1a[k], r1b[k], r1c[k]
+        return axis, (lambda p, h: s1[k].at[l, h, p]), r2a[k], r2b[k], r2c[k]
 
     def rs_copy(k, l, stage, what, di, d):
         axis, piece, ra, rb, rc = rs_parts(k, l, stage)
         pos = plane_pos[axis]
         if what == 0:
-            src, dst = piece(ring(pos, 2), di), ra.at[k, l, di]
+            src, dst = piece(ring(pos, 2), di), ra.at[l, di]
         elif what == 1:
-            src, dst = piece(ring(pos, d), 1 - di), rb.at[k, l, di]
+            src, dst = piece(ring(pos, d), 1 - di), rb.at[l, di]
         else:
-            src, dst = ra.at[k, l, di], rc.at[k, l, di]
+            src, dst = ra.at[l, di], rc.at[l, di]
         n = stage * 3 + what
         return remote(src, dst, rs_s.at[k, l, n, di], rs_r.at[k, l, n, di], {axis: ring(pos, d)})
 
@@ -362,7 +424,7 @@
         for di, d in DIRS:
             rs_copy(k, l, stage, 0, di, d).wait_recv()
             own = piece(ring(pos, d), di)
-            acc = ra.at[k, l, di]
+            acc = ra.at[l, di]
 
             def add(j, own=own, acc=acc):
                 total = (at(acc, j).astype(F32) + at(own, j).astype(F32)).astype(BF)
@@ -382,9 +444,9 @@
                 rs_copy(k, l, stage, what, di, d).wait_recv()
         for h in range(2):
             own = piece(pos, h)
-            through = rc.at[k, l, h]
-            direct = rb.at[k, l, 1 - h]
-            out = s1.at[k, l, h] if stage == 0 else s2.at[k, l, h]
+            through = rc.at[l, h]
+            direct = rb.at[l, 1 - h]
+            out = s1[k].at[l, h] if stage == 0 else s2[k].at[l, h]
 
             def add(j, own=own, through=through, direct=direct, out=out):
                 total = at(own, j).astype(F32) + at(through, j).astype(F32) + at(direct, j).astype(F32)
@@ -397,12 +459,12 @@
 
     def g_copy(k, l, di, d):
         return remote(
-            s2.at[k, l, xn_h[d]], gbuf.at[k, l, xh], g_s.at[k, l, di], g_r.at[k, l, di], to_x(xn[d])
+            s2[k].at[l, xn_h[d]], gbuf[k].at[l, xh], g_s.at[k, l, di], g_r.at[k, l, di], to_x(xn[d])
         )
 
     def ig_copy(k, l, di, d):
-        dst = ig_out.at[l, :, pl.ds(pl.multiple_of(xh * half + k * ck, ck), ck)]
-        return remote(igb.at[k, l, xn_h[d]], dst, ig_s.at[k, l, di], ig_r.at[k, l, di], to_x(xn[d]))
+        dst = ig_out.at[l, :, pl.ds(pl.multiple_of(xh * half + OFF[k], 128), WID[k])]
+        return remote(igb[k].at[l, xn_h[d]], dst, ig_s.at[k, l, di], ig_r.at[k, l, di], to_x(xn[d]))
 
     kv_core = remote(kvs, kvr, kv_s.at[0], kv_r.at[0], {CO: 1 - c})
 
@@ -426,12 +488,16 @@
         remote(nsend2, nxc.at[i], nx_s.at[i], nx_r.at[i], xc_dev(*p)) for i, p in enumerate(xc_peers)
     ]
 
-    lost = jnp.broadcast_to(failed[...], (rows, ck)) == me_r
+    def lost(shape):
+        return jnp.broadcast_to(failed[...], shape) == me_r
 
     def begin():
         loads_sp[0].wait()
         for l in range(layers):
-            spb[0, l] = spf[0, l].astype(BF)
+            spb[0, l] = spf[l].astype(BF)
+        loads_sp[1].start()
+        for cp in load_small:
+            cp.wait()
         scs[...] = jnp.broadcast_to(scale_spare[...], scs.shape)
         pl.semaphore_wait(barrier, len(plane_peers) + len(xc_peers))
         u_copy(0).start()
@@ -442,13 +508,20 @@
 
     def recover(l):
         spare_copy(0, l).wait_recv()
-        for j in range(2 * NK):
-            span = slice(j * ck, (j + 1) * ck)
-            now = jnp.where(lost, spr[0, l, :, span].astype(F32), st[0][l, :, span])
-            st[0][l, :, span] = now
-            wsb[j // NK, j % NK, l] = now.astype(BF)
-        for di, d in DIRS:
-            w_copy(l, di, d).start()
+        for h in range(2):
+            for k in range(NK + 1):
+                off, width = (OFF[k], WID[k]) if k < NK else (kept, EW // 2)
+                span = slice(h * half + off, h * half + off + width)
+                now = jnp.where(lost((rows, width)), spr[0, l, :, span].astype(F32), st[0][l, :, span])
+                st[0][l, :, span] = now
+                if k < NK:
+                    wsb[h, l, :, off : off + width] = now.astype(BF)
+                else:
+                    wbuf[NK][l, y, xh, z, :, h * width : (h + 1) * width] = now.astype(BF)
+        for k in range(NK):
+            for di, d in DIRS:
+                w_copy(k, l, di, d).start()
+        we_copy(l).start()
 
     def exchange():
         u_copy(1).start()
@@ -461,12 +534,13 @@
                     for i in (1, 2):
                         loads_sp[i].wait()
                         for ll in range(layers):
-                            spb[i, ll] = spf[i, ll].astype(BF)
+                            spb[i, ll] = spf[ll].astype(BF)
+                        if i == 1:
+                            loads_sp[2].start()
                         spare_copy(i, 0).start()
                 n += 1
         scale_copy.wait_recv()
-        lost_tile = jnp.broadcast_to(failed[...], scr.shape) == me_r
-        scr[...] = jnp.where(lost_tile, scr[...], jnp.broadcast_to(scale_own[...], scr.shape))
+        scr[...] = jnp.where(lost(scr.shape), scr[...], jnp.broadcast_to(scale_own[...], scr.shape))
         nacc[...] = jnp.zeros(nacc.shape, F32)
         load_u.wait()
         for di, d in DIRS:
@@ -487,13 +561,12 @@
                 for t in range(2):
                     ut[l, j, :, t * tok : (t + 1) * tok] = ubuf[l, t, :, span].T
 
-    got_w = set()
-
     def gather_0(k, l):
-        if l not in got_w:
-            got_w.add(l)
+        if k == NK:
+            we_copy(l).wait_recv()
+        else:
             for di, d in DIRS:
-                w_copy(l, di, d).wait_recv()
+                w_copy(k, l, di, d).wait_recv()
         for di, d in DIRS:
             ag_copy(k, l, 0, 0, di, d).start()
 
@@ -520,14 +593,31 @@
             for di, d in DIRS:
                 x_copy(k, l, di, d).wait_recv()
 
+    got_xe = set()
+
+    def need_xe():
+        if not got_xe:
+            got_xe.add(1)
+            for cp in load_xe:
+                cp.wait()
+
     def grad_product(k, l):
-        need_x(k, l)
+        if k < NK:
+            need_x(k, l)
+            width = WID[k]
+        else:
+            need_xe()
+            width = EW
 
         @pl.loop(0, 4)
         def _(j):
-            inputs = xbuf[k, l].reshape(2 * tok, ck)
-            part = jnp.dot(ut[l, j], inputs, preferred_element_type=F32)
-            dwbuf[k, l, j] = part.astype(BF).reshape(2, 4, rows, ck)
+            if k < NK:
+                inputs = xbuf[k][l].reshape(2 * tok, width)
+                part = jnp.dot(ut[l, j], inputs, preferred_element_type=F32)
+            else:
+                up = ut[l, j, :, pl.ds(pl.multiple_of(xh * tok, tok), tok)]
+                part = jnp.dot(up, xe[l], preferred_element_type=F32)
+            dwbuf[k][l, j] = part.astype(BF).reshape(2, 4, rows, width)
 
         rs_start(k, l, 0)
 
@@ -537,31 +627,52 @@
 
     got_scale = set()
 
+    def add_squares(grad):
+        nacc[:, 0 : grad.shape[1]] += grad * grad
+
     def finish_1(k, l):
         rs_finish(k, l, 1)
+        if k == NK:
+            ge_copy(l).start()
+            return
         for di, d in DIRS:
             g_copy(k, l, di, d).start()
         if not got_scale:
             got_scale.add(1)
             for di, d in DIRS:
                 sc_copy(di, d).wait_recv()
-        total = jnp.zeros((rows, ck), F32)
         for h in range(2):
-            grad = s2[k, l, h].astype(F32) / jnp.broadcast_to(scn[h, 0:1, 0:1], (rows, ck))
-            total = total + grad * grad
-        nacc[...] += total
+            add_squares(s2[k][l, h].astype(F32) / jnp.broadcast_to(scn[h, 0:1, 0:1], (rows, WID[k])))
+
+    def finish_kept(l):
+        ge_copy(l).wait_recv()
+        grad = s2[NK][l, xh].astype(F32) + grc[l].astype(F32)
+        grad = grad / jnp.broadcast_to(scr[0:1, 0:1], (rows, EW))
+        ge[l] = grad
+        add_squares(grad)
 
     kv_begun = set()
 
     def kv_product(k, l):
-        need_x(k, l)
         fresh = l not in kv_begun
         kv_begun.add(l)
+        if k == NK:
+            need_xe()
+            assert not fresh
+
+            @pl.loop(0, 4)
+            def _(j):
+                weight = wbuf[k][l, j].reshape(8 * rows, EW)
+                part = lax.dot_general(xe[l], weight, (((1,), (1,)), ((), ())), preferred_element_type=F32)
+                kvp[j, l, xh] += part
+
+            return
+        need_x(k, l)
 
         @pl.loop(0, 4)
         def _(j):
-            inputs = xbuf[k, l].reshape(2 * tok, ck)
-            weight = wbuf[k, l, j].reshape(8 * rows, ck)
+            inputs = xbuf[k][l].reshape(2 * tok, WID[k])
+            weight = wbuf[k][l, j].reshape(8 * rows, WID[k])
             part = lax.dot_general(
                 inputs, weight, (((1,), (1,)), ((), ())), preferred_element_type=F32
             ).reshape(2, tok, 8 * rows)
@@ -571,10 +682,17 @@
                 kvp[j, l] += part
 
     def ig_product(k, l):
+        if k == NK:
+            weight = wbuf[k][l].reshape(feats, EW)
+            grad = jnp.dot(ubuf[l, xh], weight, preferred_element_type=F32).astype(BF)
+            for h in range(2):
+                ig_out[l, :, h * half + kept : (h + 1) * half] = grad[:, h * (EW // 2) : (h + 1) * (EW // 2)]
+            return
+
         @pl.loop(0, 2)
         def _(t):
-            weight = wbuf[k, l].reshape(feats, ck)
-            igb[k, l, t] = jnp.dot(ubuf[l, t], weight, preferred_element_type=F32).astype(BF)
+            weight = wbuf[k][l].reshape(feats, WID[k])
+            igb[k][l, t] = jnp.dot(ubuf[l, t], weight, preferred_element_type=F32).astype(BF)
 
         for di, d in DIRS:
             ig_copy(k, l, di, d).start()
@@ -610,7 +728,7 @@
     def squares_plane():
         tile = jnp.zeros((8, 128), F32)
         for i in range(rows // 8):
-            for j in range(ck // 128):
+            for j in range(nacc.shape[1] // 128):
                 tile = tile + nacc[8 * i : 8 * i + 8, 128 * j : 128 * j + 128]
         nsend[...] = tile
         for cp in np_copies:
@@ -639,26 +757,30 @@
             total = total + nxc[i]
         squares = jnp.sum(jnp.sum(total, axis=1, keepdims=True), axis=0, keepdims=True)
         factor = jnp.minimum(1.0, lax.rsqrt(squares / entries + MEAN_EPS))
-        factor = jnp.broadcast_to(factor, (rows, ck))
-        scale = jnp.broadcast_to(scr[0:1, 0:1], (rows, ck))
-
-        @pl.loop(0, 2 * NK)
-        def _(j):
-            span = pl.ds(pl.multiple_of(j * ck, ck), ck)
-            h = j // NK
-            k = lax.rem(j, NK)
-            for l in range(layers):
-                clipped = gbuf[k, l, h].astype(F32) / scale * factor
-                first_now = jnp.where(lost, spr[1, l, :, span].astype(F32), st[1][l, :, span])
-                second_now = jnp.where(lost, spr[2, l, :, span].astype(F32), st[2][l, :, span])
-                master_now = st[0][l, :, span]
-                new_first = BETA_FIRST * first_now + (1.0 - BETA_FIRST) * clipped
-                new_second = BETA_SECOND * second_now + (1.0 - BETA_SECOND) * clipped * clipped
-                st[0][l, :, span] = master_now - LEARN_RATE * (
-                    new_first / (jnp.sqrt(new_second) + ADAM_EPS) + DECAY_RATE * master_now
-                )
-                st[1][l, :, span] = new_first
-                st[2][l, :, span] = new_second
+
+        def update(l, start, grad):
+            shape = grad.shape
+            span = slice(start, start + shape[1])
+            gone = lost(shape)
+            clipped = grad * jnp.broadcast_to(factor, shape)
+            first_now = jnp.where(gone, spr[1, l, :, span].astype(F32), st[1][l, :, span])
+            second_now = jnp.where(gone, spr[2, l, :, span].astype(F32), st[2][l, :, span])
+            master_now = st[0][l, :, span]
+            new_first = BETA_FIRST * first_now + (1.0 - BETA_FIRST) * clipped
+            new_second = BETA_SECOND * second_now + (1.0 - BETA_SECOND) * clipped * clipped
+            st[0][l, :, span] = master_now - LEARN_RATE * (
+                new_first / (jnp.sqrt(new_second) + ADAM_EPS) + DECAY_RATE * master_now
+            )
+            st[1][l, :, span] = new_first
+            st[2][l, :, span] = new_second
+
+        @pl.loop(0, layers)
+        def _(l):
+            for h in range(2):
+                for k in range(NK):
+                    scale = jnp.broadcast_to(scr[0:1, 0:1], (rows, WID[k]))
+                    update(l, h * half + OFF[k], gbuf[k][l, h].astype(F32) / scale)
+                update(l, h * half + kept, ge[l, :, h * (EW // 2) : (h + 1) * (EW // 2)])
 
     steps = {
         "INI": begin,
@@ -671,6 +793,7 @@
         "S1": gather_1,
         "F1": functools.partial(gather_forward, 1),
         "WD": gathered,
+        "FE": finish_kept,
         "DW": grad_product,
         "RF0": lambda k, l: rs_forward(k, l, 0),
         "RE0": finish_0,
@@ -702,27 +825,30 @@
     u_fwd.wait_send()
     kv_core.wait_send()
     for l in range(layers):
-        for di, d in DIRS:
-            w_copy(l, di, d).wait_send()
+        we_copy(l).wait_send()
+        ge_copy(l).wait_send()
+        for k in range(NK):
+            for di, d in DIRS:
+                w_copy(k, l, di, d).wait_send()
     for what in range(3):
         for di, d in DIRS:
             kv_copy(what, di, d).wait_send()
     for cp in np_copies + nx_copies:
         cp.wait_send()
 
-    @pl.loop(0, NK)
-    def _(k):
+    for k in range(NK + 1):
         for l in range(layers):
             for di, d in DIRS:
-                x_copy(k, l, di, d).wait_send()
-                ig_copy(k, l, di, d).wait_send()
-                g_copy(k, l, di, d).wait_send()
                 for stage in range(2):
                     for step in range(2):
                         ag_copy(k, l, stage, step, di, d).wait_send()
                     for what in range(3):
                         rs_copy(k, l, stage, what, di, d).wait_send()
-                ig_copy(k, l, di, d).wait_recv()
+                if k < NK:
+                    x_copy(k, l, di, d).wait_send()
+                    ig_copy(k, l, di, d).wait_send()
+                    g_copy(k, l, di, d).wait_send()
+                    ig_copy(k, l, di, d).wait_recv()
 
 
 def store(*refs):
@@ -750,59 +876,70 @@
     layers, tok, cols = layer_input.shape
     rows = master.shape[1]
     feats = kv_cotangent.shape[2]
-    half = cols // 2
-    ck = half // NK
     entries = float(layers * rows * lax.axis_size(FSDP) * cols * lax.axis_size(RED))
     any_ = pl.BlockSpec(memory_space=pl.ANY)
     vmem = pl.BlockSpec(memory_space=pltpu.VMEM)
     sem = pltpu.SemaphoreType.DMA
+    every = WID + (EW,)
+
+    def per_chunk(shape, widths):
+        return [pltpu.VMEM((*shape, w), BF) for w in widths]
+
     scratch = [
-        pltpu.VMEM((NK, layers, 2, tok, ck), BF),
+        per_chunk((layers, 2, tok), WID),
+        pltpu.VMEM((layers, tok, EW), BF),
         pltpu.VMEM((layers, 2, tok, feats), BF),
         pltpu.VMEM((layers, 4, feats // 4, 2 * tok), BF),
-        pltpu.VMEM((2, NK, layers, rows, ck), BF),
-        pltpu.VMEM((NK, layers, 4, 2, 4, rows, ck), BF),
-        pltpu.VMEM((NK, layers, 4, 2, 4, rows, ck), BF),
-        pltpu.VMEM((NK, layers, 2, 4, rows, ck), BF),
-        pltpu.VMEM((NK, layers, 2, 4, rows, ck), BF),
-        pltpu.VMEM((NK, layers, 2, 4, rows, ck), BF),
-        pltpu.VMEM((NK, layers, 2, 4, rows, ck), BF),
-        pltpu.VMEM((NK, layers, 2, rows, ck), BF),
-        pltpu.VMEM((NK, layers, 2, rows, ck), BF),
-        pltpu.VMEM((NK, layers, 2, rows, ck), BF),
-        pltpu.VMEM((NK, layers, 2, rows, ck), BF),
-        pltpu.VMEM((NK, layers, 2, rows, ck), BF),
-        pltpu.VMEM((NK, layers, 2, tok, ck), BF),
+        pltpu.VMEM((2, layers, rows, cols // 2 - EW // 2), BF),
+        per_chunk((layers, 4, 2, 4, rows), every),
+        per_chunk((layers, 4, 2, 4, rows), every),
+        per_chunk((layers, 2, 4, rows), every),
+        per_chunk((layers, 2, 4, rows), every),
+        per_chunk((layers, 2, 4, rows), every),
+        per_chunk((layers, 2, 4, rows), every),
+        per_chunk((layers, 2, rows), every),
+        per_chunk((layers, 2, rows), every),
+        per_chunk((layers, 2, rows), every),
+        per_chunk((layers, 2, rows), every),
+        per_chunk((layers, 2, rows), WID),
+        pltpu.VMEM((layers, rows, EW), BF),
+        pltpu.VMEM((layers, rows, EW), F32),
+        per_chunk((layers, 2, tok), WID),
         pltpu.VMEM((4, layers, 2, tok, feats // 4), F32),
         pltpu.VMEM((2, layers, 2, tok, feats // 4), BF),
         pltpu.VMEM((2, layers, 2, tok, feats // 4), BF),
         pltpu.VMEM((2, tok, feats // 4), BF),
         pltpu.VMEM((2, tok, feats // 4), BF),
         pltpu.VMEM((2, tok, feats // 4), BF),
-        pltpu.VMEM((3, layers, rows, cols), F32),
+        pltpu.VMEM((layers, rows, cols), F32),
         pltpu.VMEM((3, layers, rows, cols), BF),
         pltpu.VMEM((3, layers, rows, cols), BF),
+        [pltpu.VMEM((1, 1), jnp.int32), pltpu.VMEM((1, 1), F32), pltpu.VMEM((1, 1), F32)],
         pltpu.VMEM((8, 128), F32),
         pltpu.VMEM((8, 128), F32),
         pltpu.VMEM((2, 8, 128), F32),
-        pltpu.VMEM((rows, ck), F32),
+        pltpu.VMEM((rows, max(every)), F32),
         pltpu.VMEM((8, 128), F32),
         pltpu.VMEM((15, 8, 128), F32),
         pltpu.VMEM((8, 128), F32),
         pltpu.VMEM((7, 8, 128), F32),
-        sem((7,)),
+        sem((12,)),
         sem((5,)),
         sem((5,)),
         sem((3,)),
         sem((3,)),
         sem((NK, layers, 2)),
         sem((NK, layers, 2)),
-        sem((layers, 2)),
-        sem((layers, 2)),
-        sem((NK, layers, 4, 2)),
-        sem((NK, layers, 4, 2)),
-        sem((NK, layers, 6, 2)),
-        sem((NK, layers, 6, 2)),
+        sem((NK, layers, 2)),
+        sem((NK, layers, 2)),
+        sem((layers,)),
+        sem((layers,)),
+        sem((layers,)),
+        sem((layers,)),
+        sem((NK + 1, layers, 4, 2)),
+        sem((NK + 1, layers, 4, 2)),
+        sem((NK + 1, layers, 6, 2)),
+        sem((NK + 1, layers, 6, 2)),
         sem((NK, layers, 2)),
         sem((NK, layers, 2)),
         sem((NK, layers, 2)),
@@ -823,11 +960,11 @@
     held = pl.pallas_call(
         functools.partial(kernel, entries),
         out_shape=tuple(pltpu.VMEM(r.shape, r.dtype) for r in results),
-        in_specs=[any_, any_, vmem, vmem, vmem] + [any_] * 6,
+        in_specs=[any_] * 11,
         out_specs=(vmem,) * 5,
         scratch_shapes=scratch,
         compiler_params=pltpu.CompilerParams(
-            collective_id=0, has_side_effects=True, vmem_limit_bytes=55 << 20
+            collective_id=0, has_side_effects=True, vmem_limit_bytes=56 << 20
         ),
         name="restore_step",
     )(

time: 147 us -> 144 us (0.980)
  Pallas kernels: 145 us -> 140 us
    pallas_call x1, Pallas kernels: 142 us -> 137 us  [local(): pl.pallas_call(functools.partial(kernel, entries), out_shape=tuple((pltpu...]
where the time goes in v4:
time: 144 us; the launch traced here: 143 us
  Pallas kernels  140 us (97%)
  between operations  2.58 us (2%)
    pallas_call x1, Pallas kernels, local(): pl.pallas_call(functools.partial(kernel, entries), out_shape=tuple((pltpu...  137 us
    pallas_call x1, Pallas kernels, local(): pl.pallas_call(store, out_shape=results, in_specs=[vmem] * 5, out_specs=(...  3.11 us

profile of v4, /device:TPU:1, one launch (start us, length us, event | category | flops | bytes accessed | tf_op | source)
XLA Modules:
  0.0 143.1 jit_solution(3225525133029994625)
XLA Ops:
  2.6 137.4 %restore_step.1 = (bf16[2,256,256]{2,1,0:T(8,128)(2,1)S(1)}, bf16[2,256,4096]{2,1,0:T(8,128)(2,1)S(1)}, f32[2,32,4096]{2,1,0:T(8,128)S(1)}, f32[2,32,4096]{2,1,0:T(8,128)S(1)}, f32[2,32,4096]{2,1,0:T(8,128)S(1)}) custom-call(bf16[2,256,4096]{2,1,0:T(8,128)(2,1)} %x_in.1, bf16[2,256,1024]{2,1,0:T(8,128)(2,1)} %u_in.1, s32[1,1]{1,0:T(1,128)} %bitcast.1.failed_in, ...), custom_call_target="tpu_custom_call" | custom-call | tf_op jit(solution)/shard_map/restore_step/pallas_call | solution.py:960
  139.9 3.1 %store_results.1 = (bf16[2,256,256]{2,1,0:T(8,128)(2,1)}, bf16[2,256,4096]{2,1,0:T(8,128)(2,1)}, f32[2,32,4096]{2,1,0:T(8,128)}, f32[2,32,4096]{2,1,0:T(8,128)}, f32[2,32,4096]{2,1,0:T(8,128)}) custom-call(bf16[2,256,256]{2,1,0:T(8,128)(2,1)S(1)} %get-tuple-element.10.refs_0_, bf16[2,256,4096]{2,1,0:T(8,128)(2,1)S(1)} %get-tuple-element.11.refs_1_, ...), custom_call_target="tpu_custom_call" | custom-call | tf_op jit(solution)/shard_map/store_results/pallas_call | solution.py:983

commit v5 on v4

--- a/solution.py
+++ b/solution.py
@@ -21,139 +21,140 @@
 MEAN_EPS = 1e-06
 
 NK = 4
-WID = (512, 512, 512, 256)
+WID = (512, 512, 384, 256)
 OFF = tuple(sum(WID[:k]) for k in range(NK))
-EW = 512
-SPARES_AT = 0
+EW = 768
+SPARES_AT = 1
 ORDER = (
     ("INI",),
+    ("TR0",),
+    ("DW", 4, 1),
+    ("DW", 4, 0),
     ("WSEL", 0),
     ("WSEL", 1),
     ("XREST",),
+    ("RF0", 4, 1),
     ("A1", 0, 0),
+    ("A1", 2, 0),
     ("A1", 1, 0),
-    ("A1", 2, 0),
     ("A1", 3, 0),
+    ("RF0", 4, 0),
     ("A1", 4, 0),
+    ("A1", 1, 1),
+    ("A1", 3, 1),
+    ("A1", 0, 1),
+    ("A1", 2, 1),
+    ("RE0", 4, 1),
     ("F0", 0, 0),
-    ("A1", 0, 1),
-    ("A1", 1, 1),
-    ("A1", 2, 1),
-    ("A1", 3, 1),
-    ("F0", 1, 0),
+    ("RE0", 4, 0),
     ("A1", 4, 1),
     ("F0", 2, 0),
+    ("F0", 1, 1),
+    ("F0", 1, 0),
+    ("F0", 3, 1),
     ("F0", 3, 0),
     ("F0", 0, 1),
     ("UF",),
+    ("F0", 2, 1),
     ("F0", 4, 0),
-    ("F0", 1, 1),
     ("S1", 0, 0),
+    ("RF1", 4, 1),
+    ("TR",),
+    ("RF1", 4, 0),
+    ("S1", 2, 0),
+    ("F0", 4, 1),
     ("S1", 1, 0),
-    ("F0", 2, 1),
-    ("S1", 2, 0),
-    ("TR",),
-    ("F0", 4, 1),
+    ("S1", 3, 0),
+    ("S1", 1, 1),
+    ("S1", 3, 1),
     ("S1", 4, 0),
-    ("F0", 3, 1),
     ("S1", 0, 1),
-    ("DW", 4, 1),
-    ("S1", 1, 1),
-    ("DW", 4, 0),
-    ("S1", 3, 0),
+    ("S1", 2, 1),
+    ("RE1", 4, 0),
+    ("F1", 0, 0),
     ("DW", 0, 0),
-    ("F1", 0, 0),
+    ("F1", 1, 1),
+    ("RE1", 4, 1),
+    ("F1", 3, 1),
+    ("F1", 2, 0),
+    ("S1", 4, 1),
     ("F1", 0, 1),
-    ("RF0", 4, 1),
+    ("DW", 0, 1),
     ("F1", 1, 0),
-    ("S1", 2, 1),
-    ("DW", 0, 1),
-    ("F1", 2, 0),
-    ("F1", 1, 1),
-    ("S1", 4, 1),
     ("DW", 1, 0),
+    ("F1", 2, 1),
+    ("F1", 3, 0),
+    ("WD", 1, 1),
+    ("IG", 1, 1),
+    ("DW", 1, 1),
+    ("WD", 3, 1),
+    ("KV", 1, 1),
+    ("DW", 2, 0),
+    ("F1", 4, 0),
+    ("DW", 2, 1),
+    ("WD", 0, 0),
+    ("F1", 4, 1),
+    ("IG", 0, 0),
+    ("KV", 0, 0),
+    ("DW", 3, 0),
     ("WD", 0, 1),
+    ("RF0", 0, 0),
     ("IG", 0, 1),
     ("KV", 0, 1),
-    ("F1", 4, 0),
-    ("RE0", 4, 1),
-    ("S1", 3, 1),
-    ("DW", 1, 1),
-    ("RF0", 4, 0),
-    ("F1", 2, 1),
-    ("DW", 2, 0),
     ("RF0", 0, 1),
-    ("F1", 3, 0),
-    ("RF0", 0, 0),
-    ("DW", 2, 1),
-    ("WD", 1, 1),
-    ("IG", 1, 1),
-    ("KV", 1, 1),
-    ("DW", 3, 0),
-    ("WD", 0, 0),
-    ("IG", 0, 0),
-    ("KV", 0, 0),
-    ("F1", 4, 1),
+    ("DW", 3, 1),
+    ("KV", 3, 1),
+    ("FE", 0),
+    ("WD", 2, 0),
+    ("IG", 2, 0),
+    ("KV", 2, 0),
+    ("FE", 1),
+    ("WD", 2, 1),
+    ("IG", 2, 1),
     ("WD", 1, 0),
     ("IG", 1, 0),
-    ("DW", 3, 1),
-    ("F1", 3, 1),
-    ("WD", 2, 0),
-    ("IG", 2, 0),
+    ("KV", 2, 1),
     ("KV", 1, 0),
     ("RF0", 1, 1),
     ("RF0", 1, 0),
-    ("KV", 2, 0),
-    ("WD", 2, 1),
-    ("IG", 2, 1),
-    ("WD", 4, 0),
-    ("RF1", 4, 1),
-    ("IG", 4, 0),
-    ("RE0", 0, 1),
-    ("KV", 4, 0),
-    ("RE0", 4, 0),
+    ("WD", 3, 0),
+    ("KV", 3, 0),
     ("RF0", 2, 1),
-    ("KV", 2, 1),
     ("RF0", 2, 0),
     ("WD", 4, 1),
     ("IG", 4, 1),
-    ("WD", 3, 0),
     ("KV", 4, 1),
+    ("RE0", 0, 1),
+    ("WD", 4, 0),
+    ("RF0", 3, 0),
+    ("IG", 4, 0),
     ("RF0", 3, 1),
-    ("KV", 3, 0),
+    ("KV", 4, 0),
     ("RE0", 0, 0),
-    ("WD", 3, 1),
-    ("KV", 3, 1),
     ("KVC",),
-    ("RF0", 3, 0),
     ("RE0", 1, 1),
-    ("RF1", 4, 0),
     ("RE0", 1, 0),
-    ("RE1", 4, 1),
-    ("KVA",),
-    ("RF1", 0, 1),
     ("RE0", 2, 1),
     ("RE0", 3, 1),
+    ("RE0", 2, 0),
+    ("KVA",),
     ("RF1", 0, 0),
-    ("FE", 1),
-    ("RE0", 2, 0),
-    ("RE1", 4, 0),
+    ("RF1", 1, 0),
+    ("RF1", 0, 1),
     ("RE0", 3, 0),
-    ("RF1", 1, 0),
-    ("KVF",),
+    ("RF1", 2, 0),
     ("RF1", 1, 1),
     ("RE1", 0, 0),
-    ("RE1", 0, 1),
-    ("RF1", 2, 0),
     ("RF1", 2, 1),
+    ("RE1", 1, 0),
     ("RF1", 3, 0),
     ("RF1", 3, 1),
-    ("RE1", 1, 0),
+    ("KVF",),
+    ("RE1", 2, 0),
+    ("RE1", 0, 1),
     ("RE1", 1, 1),
-    ("RE1", 2, 0),
-    ("FE", 0),
+    ("RE1", 3, 0),
     ("RE1", 2, 1),
-    ("RE1", 3, 0),
     ("RE1", 3, 1),
     ("SQ",),
     ("KVE",),
@@ -205,7 +206,6 @@
     ge,
     igb,
     kvp,
-    kvs,
     kvr,
     ka,
     kb,
@@ -362,7 +362,7 @@
     u_far = lax.rem(x + 1 + 2 * (1 - lax.rem(x, 2)), 4)
 
     def u_copy(part):
-        span = slice(part * (tok // 2), (part + 1) * (tok // 2))
+        span = slice(0, tok // 4) if part == 0 else slice(tok // 4, tok)
         return remote(u_in.at[c, span], ubuf.at[c, xh, span], u_s.at[part], u_r.at[part], to_x(u_far))
 
     u_fwd = remote(ubuf.at[c, 1 - xh], ubuf.at[c, 1 - xh], u_s.at[2], u_r.at[2], {CO: 1 - c})
@@ -466,10 +466,12 @@
         dst = ig_out.at[l, :, pl.ds(pl.multiple_of(xh * half + OFF[k], 128), WID[k])]
         return remote(igb[k].at[l, xn_h[d]], dst, ig_s.at[k, l, di], ig_r.at[k, l, di], to_x(xn[d]))
 
-    kv_core = remote(kvs, kvr, kv_s.at[0], kv_r.at[0], {CO: 1 - c})
+    quarter = feats // 4
+    kv_core = remote(xbuf[0], kvr, kv_s.at[0], kv_r.at[0], {CO: 1 - c})
 
     def kv_piece(v, l):
-        return kvr.at[lax.rem(v, 2), l, v // 2]
+        span = pl.ds(pl.multiple_of(lax.rem(v, 2) * quarter, quarter), quarter)
+        return kvr.at[l, v // 2, :, span]
 
     def kv_copy(what, di, d):
         if what == 0:
@@ -542,7 +544,6 @@
         scale_copy.wait_recv()
         scr[...] = jnp.where(lost(scr.shape), scr[...], jnp.broadcast_to(scale_own[...], scr.shape))
         nacc[...] = jnp.zeros(nacc.shape, F32)
-        load_u.wait()
         for di, d in DIRS:
             sc_copy(di, d).start()
 
@@ -551,15 +552,21 @@
             u_copy(part).wait_recv()
         u_fwd.start()
 
-    def transpose_u():
-        u_fwd.wait_recv()
+    def transpose_u(of):
         for l in range(layers):
 
             @pl.loop(0, 4)
             def _(j):
                 span = pl.ds(pl.multiple_of(j * (feats // 4), feats // 4), feats // 4)
-                for t in range(2):
-                    ut[l, j, :, t * tok : (t + 1) * tok] = ubuf[l, t, :, span].T
+                ut[l, j, of] = ubuf[l, of, :, span].T
+
+    def transpose_own():
+        load_u.wait()
+        transpose_u(xh)
+
+    def transpose_far():
+        u_fwd.wait_recv()
+        transpose_u(1 - xh)
 
     def gather_0(k, l):
         if k == NK:
@@ -613,10 +620,10 @@
         def _(j):
             if k < NK:
                 inputs = xbuf[k][l].reshape(2 * tok, width)
-                part = jnp.dot(ut[l, j], inputs, preferred_element_type=F32)
+                up = jnp.concatenate([ut[l, j, 0], ut[l, j, 1]], axis=1)
+                part = jnp.dot(up, inputs, preferred_element_type=F32)
             else:
-                up = ut[l, j, :, pl.ds(pl.multiple_of(xh * tok, tok), tok)]
-                part = jnp.dot(up, xe[l], preferred_element_type=F32)
+                part = jnp.dot(ut[l, j, xh], xe[l], preferred_element_type=F32)
             dwbuf[k][l, j] = part.astype(BF).reshape(2, 4, rows, width)
 
         rs_start(k, l, 0)
@@ -699,14 +706,15 @@
 
     def kv_cores():
         for v in range(2):
-            kvs[v] = kvp[2 * v + (1 - c)].astype(BF)
+            xbuf[0][:, :, :, v * quarter : (v + 1) * quarter] = kvp[2 * v + (1 - c)].astype(BF)
         kv_core.start()
 
     def kv_ring():
         kv_core.wait_recv()
         for v in range(2):
             for l in range(layers):
-                kvr[v, l] = (kvr[v, l].astype(F32) + kvp[2 * v + c, l]).astype(BF)
+                span = slice(v * quarter, (v + 1) * quarter)
+                kvr[l, :, :, span] = (kvr[l, :, :, span].astype(F32) + kvp[2 * v + c, l]).astype(BF)
         for what in (0, 1):
             for di, d in DIRS:
                 kv_copy(what, di, d).start()
@@ -787,7 +795,8 @@
         "WSEL": recover,
         "XREST": exchange,
         "UF": forward_u,
-        "TR": transpose_u,
+        "TR0": transpose_own,
+        "TR": transpose_far,
         "A1": gather_0,
         "F0": functools.partial(gather_forward, 0),
         "S1": gather_1,
@@ -889,7 +898,7 @@
         per_chunk((layers, 2, tok), WID),
         pltpu.VMEM((layers, tok, EW), BF),
         pltpu.VMEM((layers, 2, tok, feats), BF),
-        pltpu.VMEM((layers, 4, feats // 4, 2 * tok), BF),
+        pltpu.VMEM((layers, 4, 2, feats // 4, tok), BF),
         pltpu.VMEM((2, layers, rows, cols // 2 - EW // 2), BF),
         per_chunk((layers, 4, 2, 4, rows), every),
         per_chunk((layers, 4, 2, 4, rows), every),
@@ -906,8 +915,7 @@
         pltpu.VMEM((layers, rows, EW), F32),
         per_chunk((layers, 2, tok), WID),
         pltpu.VMEM((4, layers, 2, tok, feats // 4), F32),
-        pltpu.VMEM((2, layers, 2, tok, feats // 4), BF),
-        pltpu.VMEM((2, layers, 2, tok, feats // 4), BF),
+        pltpu.VMEM((layers, 2, tok, feats // 2), BF),
         pltpu.VMEM((2, tok, feats // 4), BF),
         pltpu.VMEM((2, tok, feats // 4), BF),
         pltpu.VMEM((2, tok, feats // 4), BF),

time: 144 us -> 138 us (0.958)
  Pallas kernels: 140 us -> 135 us
    pallas_call x1, Pallas kernels: 137 us -> 132 us  [local(): pl.pallas_call(functools.partial(kernel, entries), out_shape=tuple((pltpu...]
where the time goes in v5:
time: 138 us
  Pallas kernels  135 us (98%)
  between operations  2.58 us (2%)
    pallas_call x1, Pallas kernels, local(): pl.pallas_call(functools.partial(kernel, entries), out_shape=tuple((pltpu...  132 us
    pallas_call x1, Pallas kernels, local(): pl.pallas_call(store, out_shape=results, in_specs=[vmem] * 5, out_specs=(...  3.11 us

profile of v5, /device:TPU:1, one launch (start us, length us, event | category | flops | bytes accessed | tf_op | source)
XLA Modules:
  0.0 137.9 jit_solution(5313925078242604180)
XLA Ops:
  2.6 132.2 %restore_step.1 = (bf16[2,256,256]{2,1,0:T(8,128)(2,1)S(1)}, bf16[2,256,4096]{2,1,0:T(8,128)(2,1)S(1)}, f32[2,32,4096]{2,1,0:T(8,128)S(1)}, f32[2,32,4096]{2,1,0:T(8,128)S(1)}, f32[2,32,4096]{2,1,0:T(8,128)S(1)}) custom-call(bf16[2,256,4096]{2,1,0:T(8,128)(2,1)} %x_in.1, bf16[2,256,1024]{2,1,0:T(8,128)(2,1)} %u_in.1, s32[1,1]{1,0:T(1,128)} %bitcast.1.failed_in, ...), custom_call_target="tpu_custom_call" | custom-call | tf_op jit(solution)/shard_map/restore_step/pallas_call | solution.py:968
  134.8 3.1 %store_results.1 = (bf16[2,256,256]{2,1,0:T(8,128)(2,1)}, bf16[2,256,4096]{2,1,0:T(8,128)(2,1)}, f32[2,32,4096]{2,1,0:T(8,128)}, f32[2,32,4096]{2,1,0:T(8,128)}, f32[2,32,4096]{2,1,0:T(8,128)}) custom-call(bf16[2,256,256]{2,1,0:T(8,128)(2,1)S(1)} %get-tuple-element.10.refs_0_, bf16[2,256,4096]{2,1,0:T(8,128)(2,1)S(1)} %get-tuple-element.11.refs_1_, ...), custom_call_target="tpu_custom_call" | custom-call | tf_op jit(solution)/shard_map/store_results/pallas_call | solution.py:991

commit v6 on v5

--- a/solution.py
+++ b/solution.py
@@ -131,6 +131,7 @@
     ("RF0", 3, 1),
     ("KV", 4, 0),
     ("RE0", 0, 0),
+    ("IG", 3, 1),
     ("KVC",),
     ("RE0", 1, 1),
     ("RE0", 1, 0),
@@ -159,7 +160,6 @@
     ("SQ",),
     ("KVE",),
     ("NX",),
-    ("IG", 3, 1),
     ("IG", 3, 0),
     ("AD",),
     ("END",),
@@ -325,8 +325,11 @@
         return {XH: v // 2, XL: lax.rem(v, 2), CO: lax.rem(c + dc, 2)}
 
     barrier = pltpu.get_barrier_semaphore()
-    for p in plane_peers:
-        pl.semaphore_signal(barrier, inc=1, device_id=plane_dev(*p), device_id_type=MESH_ID)
+    for axis in (Y, Z):
+        for _, d in DIRS:
+            pl.semaphore_signal(
+                barrier, inc=1, device_id={axis: ring(plane_pos[axis], d)}, device_id_type=MESH_ID
+            )
     for p in xc_peers:
         pl.semaphore_signal(barrier, inc=1, device_id=xc_dev(*p), device_id_type=MESH_ID)
 
@@ -501,7 +504,7 @@
         for cp in load_small:
             cp.wait()
         scs[...] = jnp.broadcast_to(scale_spare[...], scs.shape)
-        pl.semaphore_wait(barrier, len(plane_peers) + len(xc_peers))
+        pl.semaphore_wait(barrier, 4 + len(xc_peers))
         u_copy(0).start()
         for l in range(layers):
             spare_copy(0, l).start()

time: 138 us -> 138 us (level)
  no operation moved by 1% of the time
where the time goes in v6:
time: 138 us; the launch traced here: 137 us
  Pallas kernels  135 us (98%)
  between operations  2.58 us (2%)
    pallas_call x1, Pallas kernels, local(): pl.pallas_call(functools.partial(kernel, entries), out_shape=tuple((pltpu...  132 us
    pallas_call x1, Pallas kernels, local(): pl.pallas_call(store, out_shape=results, in_specs=[vmem] * 5, out_specs=(...  3.11 us

profile of v6, /device:TPU:1, one launch (start us, length us, event | category | flops | bytes accessed | tf_op | source)
XLA Modules:
  0.0 137.5 jit_solution(1988130458712871149)
XLA Ops:
  2.6 131.8 %restore_step.1 = (bf16[2,256,256]{2,1,0:T(8,128)(2,1)S(1)}, bf16[2,256,4096]{2,1,0:T(8,128)(2,1)S(1)}, f32[2,32,4096]{2,1,0:T(8,128)S(1)}, f32[2,32,4096]{2,1,0:T(8,128)S(1)}, f32[2,32,4096]{2,1,0:T(8,128)S(1)}) custom-call(bf16[2,256,4096]{2,1,0:T(8,128)(2,1)} %x_in.1, bf16[2,256,1024]{2,1,0:T(8,128)(2,1)} %u_in.1, s32[1,1]{1,0:T(1,128)} %bitcast.1.failed_in, ...), custom_call_target="tpu_custom_call" | custom-call | tf_op jit(solution)/shard_map/restore_step/pallas_call | solution.py:971
  134.4 3.1 %store_results.1 = (bf16[2,256,256]{2,1,0:T(8,128)(2,1)}, bf16[2,256,4096]{2,1,0:T(8,128)(2,1)}, f32[2,32,4096]{2,1,0:T(8,128)}, f32[2,32,4096]{2,1,0:T(8,128)}, f32[2,32,4096]{2,1,0:T(8,128)}) custom-call(bf16[2,256,256]{2,1,0:T(8,128)(2,1)S(1)} %get-tuple-element.10.refs_0_, bf16[2,256,4096]{2,1,0:T(8,128)(2,1)S(1)} %get-tuple-element.11.refs_1_, ...), custom_call_target="tpu_custom_call" | custom-call | tf_op jit(solution)/shard_map/store_results/pallas_call | solution.py:994
